TPU v7x, 32 devices: a whole 2x2x4 slice. The times are simulated.
32 devices in a mesh: group: 2 (over y), expert: 4 (over z), head: 4 (over x, core).
Axes of the slice: x: 2, y: 2, z: 4, core: 2. Of those that a mesh axis runs over, the one named last changes fastest.
Arguments:
- residual_in: bfloat16 [1024, 2048], P(('group', 'expert'), 'head'), parts along dimension 0, may hold values from -5.1 to 5.1
- norm_gain: bfloat16 [2048], P('head'), may hold values from 0.29882812 to 3
- expert_ids: int32 [1024, 8], P(('group', 'expert')), parts along dimension 0, may hold values from 0 to 63, as said below
- route_scores: float32 [1024, 8], P(('group', 'expert')), parts along dimension 0, may hold values from -0.4 to 2.2
- gate_weight: bfloat16 [64, 2048, 1024], P('expert', None, 'head'), may hold values from -0.125 to 0.125
- up_weight: bfloat16 [64, 2048, 1024], P('expert', None, 'head'), may hold values from -0.125 to 0.125
- down_weight: bfloat16 [64, 1024, 2048], P('expert', 'head'), may hold values from -0.1875 to 0.1875
- gate_exp: int32 [64, 16, 8], P('expert', None, 'head'), may hold values from -2 to 1
- up_exp: int32 [64, 16, 8], P('expert', None, 'head'), may hold values from -2 to 1
- down_exp: int32 [64, 8, 16], P('expert', 'head'), may hold values from -2 to 1
Outputs:
- mixed: bfloat16 [1024, 2048], P(('group', 'expert'), 'head'), parts along dimension 0
There are 2 independent parts, one for each index of `group`. A program takes and returns all parts, laid end to end along the dimension named above; an argument that names none is the same for every part. Nothing has to cross between parts.
Inputs may be any that keep to these rules, and one draw needn't show every extreme that they name: `expert_ids`: each row names 8 different experts. In the rows of one aligned block of 128 tokens no expert is named more than 24 times, and in every block at least one expert (up to five) is named exactly 24 times.
All inputs are finite; a program needn't handle non-finite values.
Results may differ from a plain program's by a relative error of at most 0.014.
Values may be sent and summed in bfloat16 or wider, within the bound.
No kernel may reach another device: no remote copies, remote signals or barrier semaphores. Data moves between devices by JAX's collectives and lax.ppermute only.
A program may use at most 192 MiB of HBM per device.

v0:
```python
import jax
import jax.numpy as jnp
from jax import lax
from jax.sharding import PartitionSpec as P

D = 2048
QB = 128
CAP = 24


EPSILON = 1e-06


def power_two(exponent):
    magnitude = jnp.left_shift(jnp.ones_like(exponent), jnp.abs(exponent)).astype(jnp.float32)
    return jnp.where(exponent >= 0, magnitude, 1.0 / magnitude)


def dequantize(weight, exponent, block_size):
    experts_here, row_count, col_count = weight.shape
    factor = power_two(exponent).astype(jnp.bfloat16)
    shaped = weight.reshape(
        experts_here, row_count // block_size, block_size, col_count // block_size, block_size
    )
    return (shaped * factor[:, :, None, :, None]).reshape(experts_here, row_count, col_count)


def route_tables(expert_ids, route_scores, expert_total, capacity):
    tokens_here, chosen_count = expert_ids.shape
    flat_ids = expert_ids.reshape(-1)
    onehot = (flat_ids[:, None] == jnp.arange(expert_total, dtype=jnp.int32)[None, :]).astype(
        jnp.int32
    )
    earlier = jnp.cumsum(onehot, axis=0) - onehot
    within = jnp.sum(earlier * onehot, axis=1)
    target = (flat_ids * capacity + within).reshape(tokens_here, chosen_count)
    matches = (
        target[:, :, None] == jnp.arange(expert_total * capacity, dtype=jnp.int32)[None, None, :]
    )
    raised = jnp.exp(route_scores)
    weights = (raised / jnp.sum(raised, axis=1, keepdims=True)).astype(jnp.bfloat16)
    scatter_rows = jnp.any(matches, axis=1).astype(jnp.bfloat16)
    combine_rows = jnp.sum(
        jnp.where(matches, weights[:, :, None], jnp.zeros((), jnp.bfloat16)), axis=1
    )
    return (scatter_rows, combine_rows)


def on_device(
    residual_in,
    norm_gain,
    expert_ids,
    route_scores,
    gate_weight,
    up_weight,
    down_weight,
    gate_exp,
    up_exp,
    down_exp,
):
    expert_count = lax.axis_size("expert")
    local_experts = gate_weight.shape[0]
    hidden_here = gate_weight.shape[2]
    scatter_rows, combine_rows = route_tables(
        expert_ids, route_scores, local_experts * expert_count, CAP
    )
    joined = jnp.concatenate(
        (dequantize(gate_weight, gate_exp, QB), dequantize(up_weight, up_exp, QB)), axis=2
    )
    down_full = dequantize(down_weight, down_exp, QB)
    own_values = residual_in.astype(jnp.float32)
    full_rows, full_gain = (
        lax.all_gather(residual_in, "head", axis=1, tiled=True),
        lax.all_gather(norm_gain, "head", axis=0, tiled=True),
    )
    values = full_rows.astype(jnp.float32)
    square = jnp.mean(values * values, axis=1, keepdims=True)
    normed = (values * lax.rsqrt(square + EPSILON) * full_gain.astype(jnp.float32)).astype(
        jnp.bfloat16
    )
    outgoing = jnp.einsum(
        "ts,td->sd", scatter_rows, normed, preferred_element_type=jnp.float32
    ).astype(jnp.bfloat16)
    outgoing = outgoing.reshape(expert_count, local_experts, CAP, D)
    arrived = lax.all_to_all(outgoing, "expert", split_axis=0, concat_axis=0, tiled=True)
    projected = jnp.einsum("secd,edf->secf", arrived, joined, preferred_element_type=jnp.float32)
    gate_out = projected[..., :hidden_here]
    up_out = projected[..., hidden_here:]
    activation = (jax.nn.silu(gate_out) * up_out).astype(jnp.bfloat16)
    partial_value = jnp.einsum(
        "secf,efd->secd", activation, down_full, preferred_element_type=jnp.float32
    )
    summed = lax.psum_scatter(
        partial_value.astype(jnp.bfloat16), "head", scatter_dimension=3, tiled=True
    ).astype(jnp.float32)
    returned = lax.all_to_all(
        summed.astype(jnp.bfloat16), "expert", split_axis=0, concat_axis=0, tiled=True
    ).astype(summed.dtype)
    combined = jnp.dot(
        combine_rows.astype(jnp.float32),
        returned.reshape(-1, returned.shape[3]),
        precision=lax.Precision.HIGHEST,
    )
    return (own_values + combined).astype(jnp.bfloat16)


def solution(mesh):
    placed = (
        P(("group", "expert"), "head"),
        P("head"),
        P(("group", "expert"), None),
        P(("group", "expert"), None),
        P("expert", None, "head"),
        P("expert", None, "head"),
        P("expert", "head", None),
        P("expert", None, "head"),
        P("expert", None, "head"),
        P("expert", "head", None),
    )
    return jax.shard_map(
        on_device,
        mesh=mesh,
        in_specs=placed,
        out_specs=P(("group", "expert"), "head"),
        check_vma=False,
    )
```

profile of v0, /device:TPU:0, one launch (start us, length us, event | category | flops | bytes accessed | tf_op | source)
XLA Modules:
  0.0 348.2 jit_solution(8826759847240799512)
XLA Ops:
  6.5 0.8 copy.49
  7.3 0.1 eq.42
  7.4 0.1 eq.38
  7.5 18.0 %reduce-window.6 = s32[64,8,128]{2,1,0:T(8,128)S(1)} reduce-window(s32[64,8,128]{2,1,0:T(8,128)S(1)} %fusion.26, s32[]{:T(128)} %constant.10.clone.1), window={size=1x1x128 pad=0_0x0_0x127_0}, to_apply=%region_0.0 | reduce-window | flops 8323072 | bytes 524292 | tf_op jit(solution)/shard_map/reduce-window
  25.5 0.1 slice.16
  25.7 0.1 copy.51
  25.9 0.1 copy.52
  26.0 0.1 broadcast_add_fusion
  26.1 0.1 fusion.25
  26.2 0.1 reduce_sum.42
  26.3 0.7 multiply_add_fusion
  27.0 0.1 copy.54
  27.1 3.1 fusion.5
  30.3 8.9 %all_gather.6 = bf16[128,2048]{1,0:T(8,128)(2,1)S(1)} all-gather(bf16[128,512]{1,0:T(8,128)(2,1)} %param.10), channel_id=1, replica_groups=mesh['group'=2,'expert'=4,'head'=4] {'head'}, dimensions={1}, use_global_device_ids=true | all-gather | bytes 655360 | tf_op jit(solution)/shard_map/all_gather | solution.py:73
  39.1 0.2 fusion.15
  39.3 0.7 reshape.56
  40.0 5.2 %all-gather = bf16[4,1,512]{2,1,0:T(2,128)(2,1)S(1)} all-gather(bf16[1,1,512]{2,1,0:T(2,128)(2,1)S(1)} %reshape.56), channel_id=1, replica_groups=mesh['group'=2,'expert'=4,'head'=4] {'head'}, dimensions={0}, use_global_device_ids=true | all-gather | bytes 5120 | tf_op jit(solution)/shard_map/all_gather | solution.py:74
  45.2 4.5 %convolution_convert_fusion = bf16[1536,2048]{1,0:T(8,128)(2,1)} fusion(pred[128,1536]{1,0:T(8,128)(4,1)S(1)} %fusion.5, bf16[128,2048]{1,0:T(8,128)(2,1)S(1)} %all_gather.6, f32[2048]{0:T(1024)S(1)} %bitcast.47, f32[128]{0:T(128)S(1)} %add_rsqrt_fusion), kind=kOutput, calls=%fused_computation.5 | convolution fusion | flops 809500672 | bytes 7021056 | tf_op jit(solution)/shard_map/ts,td->sd/dot_general | solution.py:81
  49.7 0.0 copy-start.1
  49.7 5.4 %all-to-all-start = ((bf16[4,16,24,2048]{3,2,1,0:T(8,128)(2,1)}), bf16[4,16,24,2048]{3,2,1,0:T(8,128)(2,1)}, u32[]{:S(2)}, u32[]{:S(2)}) async-start(bf16[4,16,24,2048]{3,2,1,0:T(8,128)(2,1)} %bitcast.44), calls=%async_computation | async-start | bytes 12582912 | tf_op jit(solution)/shard_map/all_to_all | solution.py:85
  55.1 0.2 reduce-scatter.2.cloned.1.call-start
  55.3 0.0 copy-done.1
  55.4 0.2 copy.56
  55.6 12.3 %mul.76 = bf16[16,16,128,2,128]{4,3,2,1,0:T(2,128)(2,1)} broadcast(bf16[16,16,2]{2,1,0:T(8,128)(2,1)S(1)} %copy.56), dimensions={0,1,3} | broadcast | bytes 16778240 | tf_op jit(solution)/shard_map/mul | solution.py:25
  67.8 0.0 copy-start.2
  67.8 26.9 %mul.77 = bf16[16,2048,256]{2,1,0:T(8,128)(2,1)} reshape(bf16[16,16,128,2,128]{4,3,2,1,0:T(2,128)(2,1)} %mul.76) | data formatting | bytes 33554432 | tf_op jit(solution)/shard_map/mul | solution.py:25
  94.7 0.0 copy-done.2
  94.8 0.2 copy.57
  95.0 12.3 %mul.79 = bf16[16,16,128,2,128]{4,3,2,1,0:T(2,128)(2,1)} broadcast(bf16[16,16,2]{2,1,0:T(8,128)(2,1)S(1)} %copy.57), dimensions={0,1,3} | broadcast | bytes 16778240 | tf_op jit(solution)/shard_map/mul | solution.py:25
  107.3 0.0 copy-start.3
  107.3 26.9 %mul.80 = bf16[16,2048,256]{2,1,0:T(8,128)(2,1)} reshape(bf16[16,16,128,2,128]{4,3,2,1,0:T(2,128)(2,1)} %mul.79) | data formatting | bytes 33554432 | tf_op jit(solution)/shard_map/mul | solution.py:25
  134.2 0.0 copy-done.3
  134.2 6.1 %mul.73 = bf16[16,2,128,16,128]{4,3,2,1,0:T(8,128)(2,1)} broadcast(bf16[16,2,16]{2,1,0:T(2,128)(2,1)S(1)} %fusion.27), dimensions={0,1,3} | broadcast | bytes 16778240 | tf_op jit(solution)/shard_map/mul | solution.py:25
  140.3 25.3 %mul.74 = bf16[16,256,2048]{2,1,0:T(8,128)(2,1)} reshape(bf16[16,2,128,16,128]{4,3,2,1,0:T(8,128)(2,1)} %mul.73) | data formatting | bytes 33554432 | tf_op jit(solution)/shard_map/mul | solution.py:25
  165.6 18.4 %mul.78 = bf16[16,2048,256]{2,1,0:T(8,128)(2,1)} multiply(bf16[16,2048,256]{2,1,0:T(8,128)(2,1)} %param.14, bf16[16,2048,256]{2,1,0:T(8,128)(2,1)} %mul.77) | non-fusion elementwise | flops 8388608 | bytes 50331648 | tf_op jit(solution)/shard_map/mul | solution.py:25
  184.0 18.4 %mul.81 = bf16[16,2048,256]{2,1,0:T(8,128)(2,1)} multiply(bf16[16,2048,256]{2,1,0:T(8,128)(2,1)} %param.15, bf16[16,2048,256]{2,1,0:T(8,128)(2,1)} %mul.80) | non-fusion elementwise | flops 8388608 | bytes 50331648 | tf_op jit(solution)/shard_map/mul | solution.py:25
  202.4 0.0 all-to-all-done
  202.4 14.1 %fusion.10 = f32[4,16,24,512]{3,2,0,1:T(8,128)S(1)} fusion(bf16[4,16,24,2048]{3,2,1,0:T(8,128)(2,1)} %all-to-all-done, bf16[16,2048,256]{2,1,0:T(8,128)(2,1)} %mul.81, bf16[16,2048,256]{2,1,0:T(8,128)(2,1)} %mul.78), kind=kOutput, calls=%fused_computation.12 | convolution fusion | flops 3288334336 | bytes 42991616 | tf_op jit(solution)/shard_map/secd,edf->secf/dot_general | solution.py:86
  216.4 20.9 %convert_bitcast_fusion = bf16[4,16,24,2048]{3,2,0,1:T(8,128)(2,1)} fusion(bf16[16,256,2048]{2,1,0:T(8,128)(2,1)} %param.16, bf16[16,256,2048]{2,1,0:T(8,128)(2,1)} %mul.74, f32[4,16,24,512]{3,2,0,1:T(8,128)S(1)} %fusion.10), kind=kOutput, calls=%fused_computation.7 | convolution fusion | flops 1649672192 | bytes 42991616 | tf_op jit(solution)/shard_map/secf,efd->secd/dot_general | solution.py:90
  237.4 0.0 copy-start.4
  237.4 0.0 copy-start
  237.4 0.0 reduce-scatter.2.cloned.1.call-update
  237.4 58.9 %reduce-scatter.2.cloned.1.call-done = bf16[4,16,24,512]{3,2,0,1:T(8,128)(2,1)} async-done(((bf16[4,16,24,2048]{3,2,0,1:T(8,128)(2,1)}), bf16[4,16,24,512]{3,2,0,1:T(8,128)(2,1)}) %reduce-scatter.2.cloned.1.call-update) | async-done | bytes 1572880 | tf_op jit(solution)/shard_map/reduce_scatter | solution.py:93
  296.3 2.7 copy.59
  299.0 4.6 %all-to-all-start.1 = ((bf16[4,16,24,512]{3,2,1,0:T(8,128)(2,1)}), bf16[4,16,24,512]{3,2,1,0:T(8,128)(2,1)S(1)}, u32[]{:S(2)}, u32[]{:S(2)}) async-start(bf16[4,16,24,512]{3,2,1,0:T(8,128)(2,1)} %copy.59), calls=%async_computation.2 | async-start | bytes 3145728 | tf_op jit(solution)/shard_map/all_to_all | solution.py:96
  303.6 0.0 copy-done.4
  303.6 0.1 copy.55
  303.7 2.1 fusion.9
  305.8 34.5 %all-to-all-done.1 = bf16[4,16,24,512]{3,2,1,0:T(8,128)(2,1)S(1)} async-done(((bf16[4,16,24,512]{3,2,1,0:T(8,128)(2,1)}), bf16[4,16,24,512]{3,2,1,0:T(8,128)(2,1)S(1)}, u32[]{:S(2)}, u32[]{:S(2)}) %all-to-all-start.1) | async-done | bytes 1572896 | tf_op jit(solution)/shard_map/all_to_all | solution.py:96
  340.4 0.0 copy-done
  340.4 1.0 fusion.14
  (11 shorter events, 0.2 us)
Async XLA Ops:
  49.7 5.6 %copy-start.1 = (s32[16,16,2]{1,2,0:T(2,128)S(1)}, s32[16,16,2]{1,2,0:T(2,128)}, u32[]{:S(2)}) copy-start(s32[16,16,2]{1,2,0:T(2,128)} %param.17) | copy-start | bytes 6148
  49.7 152.7 %all-to-all-start = ((bf16[4,16,24,2048]{3,2,1,0:T(8,128)(2,1)}), bf16[4,16,24,2048]{3,2,1,0:T(8,128)(2,1)}, u32[]{:S(2)}, u32[]{:S(2)}) async-start(bf16[4,16,24,2048]{3,2,1,0:T(8,128)(2,1)} %bitcast.44), calls=%async_computation | async-start | bytes 12582912 | tf_op jit(solution)/shard_map/all_to_all | solution.py:85
  55.1 241.2 %reduce-scatter.2.cloned.1.call-start = ((), (), s32[]{:S(2)}) async-start(), calls=%async_computation.3 | async-start | bytes 7864320 | tf_op jit(solution)/shard_map/reduce_scatter | solution.py:93
  67.8 26.9 %copy-start.2 = (s32[16,16,2]{1,2,0:T(2,128)S(1)}, s32[16,16,2]{1,2,0:T(2,128)}, u32[]{:S(2)}) copy-start(s32[16,16,2]{1,2,0:T(2,128)} %param.18) | copy-start | bytes 6148
  107.3 26.9 %copy-start.3 = (s32[16,2,16]{2,1,0:T(2,128)S(1)}, s32[16,2,16]{2,1,0:T(2,128)}, u32[]{:S(2)}) copy-start(s32[16,2,16]{2,1,0:T(2,128)} %param.19) | copy-start | bytes 6148
  237.4 66.2 %copy-start.4 = (f32[128,8]{0,1:T(8,128)S(1)}, f32[128,8]{0,1:T(8,128)}, u32[]{:S(2)}) copy-start(f32[128,8]{0,1:T(8,128)} %param.13) | copy-start | bytes 12292
  237.4 103.0 %copy-start = (bf16[128,512]{1,0:T(8,128)(2,1)S(1)}, bf16[128,512]{1,0:T(8,128)(2,1)}, u32[]{:S(2)}) copy-start(bf16[128,512]{1,0:T(8,128)(2,1)} %param.10) | copy-start | bytes 393220
  299.0 41.4 %all-to-all-start.1 = ((bf16[4,16,24,512]{3,2,1,0:T(8,128)(2,1)}), bf16[4,16,24,512]{3,2,1,0:T(8,128)(2,1)S(1)}, u32[]{:S(2)}, u32[]{:S(2)}) async-start(bf16[4,16,24,512]{3,2,1,0:T(8,128)(2,1)} %copy.59), calls=%async_computation.2 | async-start | bytes 3145728 | tf_op jit(solution)/shard_map/all_to_all | solution.py:96
Sparse Core Ops, SparseCore 0:
  237.5 58.7 reduce-scatter.1
where the time goes:
time: 351 us; the launch traced here: 348 us
  local copies, waits for them, and re-layouts  115 us (33%)
  waiting for transfers between devices  93.4 us (27%)
  other arithmetic  61.3 us (17%)
  matrix products  40.5 us (12%)
  blocking collectives  14 us (4%)
  between operations  13.5 us (4%)
  starting transfers between devices  10.2 us (3%)
    mul x6, local copies, waits for them, and re-layouts, dequantize(): shaped * factor[:, :, None, :, None]  110 us
    reduce_scatter x1, waiting for transfers between devices, on_device(): lax.psum_scatter(partial_value.astype(jnp.bfloat16), 'head', scatter_dime...  58.9 us
    mul x2, other arithmetic, dequantize(): shaped * factor[:, :, None, :, None]  36.8 us
    all_to_all x1, waiting for transfers between devices, on_device(): lax.all_to_all(summed.astype(jnp.bfloat16), 'expert', split_axis=0, conca...  34.5 us
    dot_general x1, matrix products, on_device(): jnp.einsum('secf,efd->secd', activation, down_full, preferred_element_typ...  20.9 us
    another operation x3, other arithmetic  18.2 us
    dot_general x1, matrix products, on_device(): jnp.einsum('secd,edf->secf', arrived, joined, preferred_element_type=jnp....  14.1 us
    all_gather x1, blocking collectives, on_device(): lax.all_gather(residual_in, 'head', axis=1, tiled=True)  8.86 us
  transfers between devices with their start and end apart: 3, of which 2 were waited for; matrix products, arithmetic and copies ran while one was open for 43% of the time, Pallas kernels for 0%

commit v1 on v0

v1 whole, which is shorter than its diff:
```python
import functools

import jax
import jax.numpy as jnp
from jax import lax
from jax.experimental import pallas as pl
from jax.experimental.pallas import tpu as pltpu
from jax.sharding import PartitionSpec as P

QB = 128
CAP = 24
EXTRA = 16
EPSILON = 1e-06
MIB = 1 << 20


def power_two(exponent):
    magnitude = jnp.left_shift(jnp.ones_like(exponent), jnp.abs(exponent)).astype(jnp.float32)
    return jnp.where(exponent >= 0, magnitude, 1.0 / magnitude)


def pack_kernel(rows_ref, gain_ref, ids_ref, scores_ref, out_ref):
    tokens, width = rows_ref.shape
    top = ids_ref.shape[0]
    out_ref[:tokens, :] = rows_ref[...]
    raised = jnp.exp(scores_ref[...])
    weights = raised / jnp.sum(raised, axis=0, keepdims=True)
    routes = jnp.concatenate((ids_ref[...].astype(jnp.float32), weights), axis=1)
    if width > 2 * tokens:
        routes = jnp.concatenate((routes, jnp.zeros((top, width - 2 * tokens), jnp.float32)), axis=1)
    gain = jnp.broadcast_to(gain_ref[...].astype(jnp.float32), (EXTRA - top, width))
    out_ref[tokens:, :] = jnp.concatenate((routes, gain), axis=0).astype(jnp.bfloat16)


def scaled(block, factor):
    parts = []
    for i, value in enumerate(factor):
        piece = block[i * QB : (i + 1) * QB]
        by = jnp.full((16, QB), value, jnp.float32).astype(jnp.bfloat16)
        parts.append((piece.reshape(QB // 16, 16, QB) * by[None]).reshape(QB, QB))
    return parts[0] if len(parts) == 1 else jnp.concatenate(parts, axis=0)


def up_kernel(n_head, n_block, split, place_ref, gate_fac, up_fac, *refs):
    n_piece = n_head * n_block if split else 1
    pieces = refs[:n_piece]
    gate_ref, up_ref, act_ref, comb_ref, normed, taken, slots = refs[n_piece:]

    def piece(f, j):
        return pieces[f * n_block + j] if split else pieces[0].at[f, j]

    experts, features, hidden = gate_ref.shape
    width = features // n_head
    tokens = normed.shape[0] // n_block
    pair = 2 * tokens
    slot = 2 * CAP
    cols = hidden // QB
    top = 8
    for j in range(n_block):
        total = jnp.zeros((tokens, 1), jnp.float32)
        for f in range(n_head):
            value = piece(f, j)[:tokens, :].astype(jnp.float32)
            total = total + jnp.sum(value * value, axis=1, keepdims=True)
        scale = lax.rsqrt(total / features + EPSILON)
        for f in range(n_head):
            value = piece(f, j)[:tokens, :].astype(jnp.float32)
            gain = piece(f, j)[tokens + top : tokens + top + 8, :].astype(jnp.float32)[0:1, :]
            normed[pl.ds(j * tokens, tokens), pl.ds(f * width, width)] = (
                value * scale * gain
            ).astype(jnp.bfloat16)
    first = place_ref[n_head]
    row = lax.broadcasted_iota(jnp.int32, (pair, pair), 0)
    col = lax.broadcasted_iota(jnp.int32, (pair, pair), 1)
    before = ((row < col) & ((row >= tokens) | (col < tokens))).astype(jnp.bfloat16)
    expert = (lax.broadcasted_iota(jnp.int32, (experts, pair), 0) + first).astype(jnp.float32)
    second = lax.broadcasted_iota(jnp.int32, (experts, pair), 1) >= tokens
    slot_no = lax.broadcasted_iota(jnp.int32, (slot, pair), 0).astype(jnp.float32)
    for p in range(n_block // 2):
        lists = [piece(0, 2 * p + i)[tokens : tokens + top, : 2 * tokens].astype(jnp.float32) for i in range(2)]
        ids = jnp.concatenate([x[:, :tokens] for x in lists], axis=1)
        weights = jnp.concatenate([x[:, tokens:] for x in lists], axis=1)
        named = jnp.zeros((experts, pair), jnp.float32)
        weight = jnp.zeros((experts, pair), jnp.float32)
        for k in range(top):
            same = ids[k : k + 1, :] == expert
            named = jnp.where(same, 1.0, named)
            weight = jnp.where(same, weights[k : k + 1, :], weight)
        rank = jnp.dot(named.astype(jnp.bfloat16), before, preferred_element_type=jnp.float32)
        target = jnp.where(named > 0, rank + jnp.where(second, float(CAP), 0.0), -1.0)
        back = []
        for e in range(experts):
            here = target[e : e + 1, :] == slot_no
            taken[pl.ds(e * slot, slot), :] = jnp.where(here, 1.0, 0.0).astype(jnp.bfloat16)
            back.append(jnp.where(here, weight[e : e + 1, :], 0.0))
        comb_ref[p] = jnp.transpose(jnp.concatenate(back, axis=0)).astype(jnp.bfloat16)
        step = min(features, 256)
        for n in range(features // step):
            rows = jnp.dot(
                taken[...],
                normed[pl.ds(p * pair, pair), pl.ds(n * step, step)],
                preferred_element_type=jnp.float32,
            ).astype(jnp.bfloat16)
            slots[:, pl.ds(p * slot, slot), pl.ds(n * step, step)] = rows.reshape(experts, slot, step)

    per_piece = width // QB

    def one_expert(e, carry):
        outs = []
        for ref, fac in ((gate_ref, gate_fac), (up_ref, up_fac)):
            acc = None
            for f in range(n_head):
                start = pl.multiple_of(place_ref[f] * width, width)
                left = slots[e, :, pl.ds(f * width, width)]
                base = (e * (features // QB) + place_ref[f] * per_piece) * cols
                block = ref[e, pl.ds(start, width), :]
                right = [
                    scaled(
                        block[:, n * QB : (n + 1) * QB],
                        [fac[base + i * cols + n] for i in range(per_piece)],
                    )
                    for n in range(cols)
                ]
                right = right[0] if cols == 1 else jnp.concatenate(right, axis=1)
                term = jnp.dot(left, right, preferred_element_type=jnp.float32)
                acc = term if acc is None else acc + term
            outs.append(acc)
        gate_out, up_out = outs
        act = gate_out / (1.0 + jnp.exp(-gate_out)) * up_out
        act_ref[e] = act.astype(jnp.bfloat16)
        return carry

    lax.fori_loop(0, experts, one_expert, 0)


def down_kernel(chunks, n_head, place_ref, down_fac, act_ref, comb_ref, down_ref, *refs):
    outs, (partial,) = refs[: len(chunks)], refs[len(chunks) :]
    experts, hidden, features = down_ref.shape
    width = features // n_head
    n_pair, pair, _ = comb_ref.shape
    slot = 2 * CAP
    per_piece = width // QB
    for f, out in zip(chunks, outs):
        start = pl.multiple_of(place_ref[f] * width, width)

        def one_expert(e, carry):
            block = down_ref[e, :, pl.ds(start, width)]
            base = e * (hidden // QB) * (features // QB) + place_ref[f] * per_piece
            right = jnp.concatenate(
                [
                    scaled(
                        block[:, n * QB : (n + 1) * QB],
                        [down_fac[base + i * (features // QB) + n] for i in range(hidden // QB)],
                    )
                    for n in range(per_piece)
                ],
                axis=1,
            )
            value = jnp.dot(act_ref[e], right, preferred_element_type=jnp.float32).astype(jnp.bfloat16)
            for p in range(n_pair):
                partial[p, pl.ds(pl.multiple_of(e * slot, slot), slot), :] = value[p * slot : (p + 1) * slot]
            return carry

        lax.fori_loop(0, experts, one_expert, 0)
        for p in range(n_pair):
            out[pl.ds(p * pair, pair), :] = jnp.dot(
                comb_ref[p], partial[p], preferred_element_type=jnp.float32
            ).astype(jnp.bfloat16)


def on_device(n_expert, n_head, residual_in, norm_gain, expert_ids, route_scores,
              gate_weight, up_weight, down_weight, gate_exp, up_exp, down_exp):
    tokens, width = residual_in.shape
    experts, features, hidden = gate_weight.shape
    split = n_expert * n_head <= 16
    vmem, smem = pl.BlockSpec(memory_space=pltpu.VMEM), pl.BlockSpec(memory_space=pltpu.SMEM)
    packed = pl.pallas_call(
        pack_kernel,
        out_shape=jax.ShapeDtypeStruct((tokens + EXTRA, width), jnp.bfloat16),
        in_specs=[vmem] * 4,
        out_specs=vmem,
        compiler_params=pltpu.CompilerParams(vmem_limit_bytes=2 * MIB),
        name="pack",
    )(residual_in, norm_gain[None, :], expert_ids.T, route_scores.T)
    head, expert = lax.axis_index("head"), lax.axis_index("expert")

    def swap(value, bit):
        return lax.ppermute(value, "head", [(i, i ^ bit) for i in range(n_head)])

    def shift(value, k):
        return lax.ppermute(value, "expert", [(i, (i + k) % n_expert) for i in range(n_expert)])

    bits = [1 << i for i in range(n_head.bit_length() - 1)]
    if split:
        pieces = {0: [packed] + [shift(packed, k) for k in range(1, n_expert)]}
        for bit in reversed(bits):
            for f in list(pieces):
                pieces[f | bit] = [swap(value, bit) for value in pieces[f]]
        gathered = [value for f in range(n_head) for value in pieces[f]]
        heads = [head ^ f for f in range(n_head)]
    else:
        gathered = [lax.all_gather(lax.all_gather(packed, "expert"), "head")]
        heads = [jnp.int32(f) for f in range(n_head)]
    place = jnp.stack(heads + [expert * experts]).astype(jnp.int32)
    factors = [power_two(x).reshape(-1) for x in (gate_exp, up_exp, down_exp)]
    n_pair, pair, slot = n_expert // 2, 2 * tokens, 2 * CAP
    act, comb = pl.pallas_call(
        functools.partial(up_kernel, n_head, n_expert, split),
        out_shape=(
            jax.ShapeDtypeStruct((experts, n_pair * slot, hidden), jnp.bfloat16),
            jax.ShapeDtypeStruct((n_pair, pair, experts * slot), jnp.bfloat16),
        ),
        in_specs=[smem] * 3 + [vmem] * (len(gathered) + 2),
        out_specs=(vmem, vmem),
        scratch_shapes=[
            pltpu.VMEM((n_expert * tokens, features), jnp.bfloat16),
            pltpu.VMEM((experts * slot, pair), jnp.bfloat16),
            pltpu.VMEM((experts, n_pair * slot, features), jnp.bfloat16),
        ],
        compiler_params=pltpu.CompilerParams(vmem_limit_bytes=UP_VMEM * MIB),
        name="up",
    )(place, factors[0], factors[1], *gathered, VM(gate_weight), VM(up_weight))

    def down(chunks):
        return pl.pallas_call(
            functools.partial(down_kernel, chunks, n_head),
            out_shape=[jax.ShapeDtypeStruct((n_expert * tokens, width), jnp.bfloat16)] * len(chunks),
            in_specs=[smem] * 2 + [vmem] * 3,
            out_specs=[vmem] * len(chunks),
            scratch_shapes=[pltpu.VMEM((n_pair, experts * slot, width), jnp.bfloat16)],
            compiler_params=pltpu.CompilerParams(vmem_limit_bytes=DOWN_VMEM * MIB),
            name="down" + "".join(str(c) for c in chunks),
        )(place, factors[2], act, comb, VM(down_weight))

    def add(a, b):
        return (a.astype(jnp.float32) + b.astype(jnp.float32)).astype(jnp.bfloat16)

    own = residual_in.astype(jnp.float32)
    if split:
        order = list(range(n_head))[::-1]
        sums = dict(zip(order, down(order)))
        for bit in bits:
            for f in [f for f in list(sums) if f & bit]:
                sums[f ^ bit] = add(sums[f ^ bit], swap(sums.pop(f), bit))
        mine = sums[0].reshape(n_expert, tokens, width)
        combined = mine[0].astype(jnp.float32)
        for k in range(1, n_expert):
            combined = combined + shift(mine[n_expert - k], k).astype(jnp.float32)
    else:
        parts = jnp.stack(down(list(range(n_head))))
        mine = lax.psum_scatter(parts, "head", scatter_dimension=0)
        mine = mine.reshape(n_expert, tokens, width)
        combined = lax.psum_scatter(mine, "expert", scatter_dimension=0).astype(jnp.float32)
    return (own + combined).astype(jnp.bfloat16)


UP_VMEM = 24
DOWN_VMEM = 16


def VM(x):
    return pltpu.with_memory_space_constraint(x, pltpu.VMEM)


def solution(mesh):
    placed = (
        P(("group", "expert"), "head"),
        P("head"),
        P(("group", "expert"), None),
        P(("group", "expert"), None),
        P("expert", None, "head"),
        P("expert", None, "head"),
        P("expert", "head", None),
        P("expert", None, "head"),
        P("expert", None, "head"),
        P("expert", "head", None),
    )
    return jax.shard_map(
        functools.partial(on_device, mesh.shape["expert"], mesh.shape["head"]),
        mesh=mesh,
        in_specs=placed,
        out_specs=P(("group", "expert"), "head"),
        check_vma=False,
    )
```

time: 351 us -> 112 us (0.32)
  local copies, waits for them, and re-layouts: 115 us -> 26.4 us
  waiting for transfers between devices: 93.4 us -> 30.2 us
  other arithmetic: 61.3 us -> 3.3 us
  matrix products: 40.5 us -> 0 us
  Pallas kernels: 0 us -> 28.5 us
  blocking collectives: 14 us -> 0 us
  between operations: 13.5 us -> 0.25 us
  starting transfers between devices: 10.2 us -> 21.8 us
    mul x6 -> x0, local copies, waits for them, and re-layouts: 110 us -> none  [dequantize(): shaped * factor[:, :, None, :, None]]
    reduce_scatter x1 -> x0, waiting for transfers between devices: 58.9 us -> none  [on_device(): lax.psum_scatter(partial_value.astype(jnp.bfloat16), 'head', scatter_dime...]
    dot_general x4 -> x0, matrix products: 40.5 us -> none  [the longest x1 20.9 us: on_device(): jnp.einsum('secf,efd->secd', activation, down_full, preferred_element_typ...]
    mul x2 -> x0, other arithmetic: 36.8 us -> none  [dequantize(): shaped * factor[:, :, None, :, None]]
    all_to_all x2 -> x0, waiting for transfers between devices: 34.5 us -> none  [the longest x1 34.5 us: on_device(): lax.all_to_all(summed.astype(jnp.bfloat16), 'expert', split_axis=0, conca...]
    ppermute x0 -> x21, waiting for transfers between devices: none -> 30.2 us  [the longest x15 19.6 us: swap(): return lax.ppermute(value, 'head', [(i, i ^ bit) for i in range(n_head)])]
    pallas_call x0 -> x3, Pallas kernels: none -> 28.5 us  [the longest x1 15.2 us: down(): pl.pallas_call(functools.partial(down_kernel, chunks, n_head), out_shape=...]
    ppermute x0 -> x21, starting transfers between devices: none -> 21.8 us  [the longest x6 13.8 us: shift(): lax.ppermute(value, 'expert', [(i, (i + k) % n_expert) for i in range(n_e...]
  transfers between devices with their start and end apart: 3 -> 21, of which waited for: 2 -> 7; matrix products, arithmetic and copies ran while one was open for 43% -> 4% of each run, Pallas kernels for 0% -> 0%
where the time goes in v1:
time: 112 us; the launch traced here: 111 us
  waiting for transfers between devices  30.2 us (27%)
  Pallas kernels  28.5 us (25%)
  local copies, waits for them, and re-layouts  26.4 us (24%)
  starting transfers between devices  21.8 us (19%)
  other arithmetic  3.3 us (3%)
    unnamed x52, local copies, waits for them, and re-layouts  23.2 us
    ppermute x15, waiting for transfers between devices, swap(): return lax.ppermute(value, 'head', [(i, i ^ bit) for i in range(n_head)])  19.6 us
    pallas_call x1, Pallas kernels, down(): pl.pallas_call(functools.partial(down_kernel, chunks, n_head), out_shape=...  15.2 us
    ppermute x6, starting transfers between devices, shift(): lax.ppermute(value, 'expert', [(i, (i + k) % n_expert) for i in range(n_e...  13.8 us
    pallas_call x1, Pallas kernels, on_device(): pl.pallas_call(functools.partial(up_kernel, n_head, n_expert, split), out...  13.3 us
    ppermute x6, waiting for transfers between devices, shift(): lax.ppermute(value, 'expert', [(i, (i + k) % n_expert) for i in range(n_e...  10.6 us
    ppermute x15, starting transfers between devices, swap(): return lax.ppermute(value, 'head', [(i, i ^ bit) for i in range(n_head)])  8 us
  transfers between devices with their start and end apart: 21, of which 7 were waited for; matrix products, arithmetic and copies ran while one was open for 4% of the time, Pallas kernels for 0%

profile of v1, /device:TPU:0, one launch (start us, length us, event | category | flops | bytes accessed | tf_op | source)
XLA Modules:
  0.0 110.5 jit_solution(5744621820661476290)
XLA Ops:
  0.0 0.7 broadcast_in_dim.7.gain_ref
  0.7 0.9 copy-done.6
  1.6 0.7 copy-done.9
  2.3 0.7 copy-done.10
  3.0 3.1 %collective-permute-start = (bf16[144,512]{1,0:T(8,128)(2,1)S(1)}, bf16[144,512]{1,0:T(8,128)(2,1)S(1)}, u32[]{:S(2)}, u32[]{:S(2)}) collective-permute-start(bf16[144,512]{1,0:T(8,128)(2,1)S(1)} %pack.1.refs_0_), channel_id=1, source_target_pairs={{0,4},{4,8},{8,12},{12,0},{1,5},{5,9},{9,13},{13,1},{2,6},{6,10},{... | collective-permute-start | bytes 442376 | tf_op jit(solution)/shard_map/ppermute | solution.py:190
  6.1 2.6 %collective-permute-start.1 = (bf16[144,512]{1,0:T(8,128)(2,1)S(1)}, bf16[144,512]{1,0:T(8,128)(2,1)S(1)}, u32[]{:S(2)}, u32[]{:S(2)}) collective-permute-start(bf16[144,512]{1,0:T(8,128)(2,1)S(1)} %pack.1.refs_0_), channel_id=1, source_target_pairs={{0,8},{4,12},{8,0},{12,4},{1,9},{5,13},{9,1},{13,5},{2,10},{6,14},... | collective-permute-start | bytes 442376 | tf_op jit(solution)/shard_map/ppermute | solution.py:190
  8.7 1.3 %collective-permute-start.2 = (bf16[144,512]{1,0:T(8,128)(2,1)S(1)}, bf16[144,512]{1,0:T(8,128)(2,1)S(1)}, u32[]{:S(2)}, u32[]{:S(2)}) collective-permute-start(bf16[144,512]{1,0:T(8,128)(2,1)S(1)} %pack.1.refs_0_), channel_id=1, source_target_pairs={{0,12},{4,0},{8,4},{12,8},{1,13},{5,1},{9,5},{13,9},{2,14},{6,2},{... | collective-permute-start | bytes 442376 | tf_op jit(solution)/shard_map/ppermute | solution.py:190
  10.0 1.5 %collective-permute-start.7 = (bf16[144,512]{1,0:T(8,128)(2,1)S(1)}, bf16[144,512]{1,0:T(8,128)(2,1)S(1)}, u32[]{:S(2)}, u32[]{:S(2)}) collective-permute-start(bf16[144,512]{1,0:T(8,128)(2,1)S(1)} %pack.1.refs_0_), channel_id=1, source_target_pairs={{0,2},{1,3},{2,0},{3,1},{4,6},{5,7},{6,4},{7,5},{8,10},{9,11},{10,... | collective-permute-start | bytes 442376 | tf_op jit(solution)/shard_map/ppermute | solution.py:187
  11.5 0.0 collective-permute-start.3
  11.5 0.7 compare_select_fusion.1
  12.3 0.2 copy.11
  12.4 0.7 reshape.19.gate_fac
  13.2 0.0 collective-permute-done.refs_1_
  13.2 1.5 %collective-permute-start.8 = (bf16[144,512]{1,0:T(8,128)(2,1)S(1)}, bf16[144,512]{1,0:T(8,128)(2,1)S(1)}, u32[]{:S(2)}, u32[]{:S(2)}) collective-permute-start(bf16[144,512]{1,0:T(8,128)(2,1)S(1)} %collective-permute-done.refs_1_), channel_id=1, source_target_pairs={{0,2},{1,3},{2,0},{3,1},{4,6},{5,7},{6,4},{7,5},{8,10},{9,11},{10,... | collective-permute-start | bytes 442376 | tf_op jit(solution)/shard_map/ppermute | solution.py:187
  14.6 3.8 %collective-permute-done.1.refs_2_ = bf16[144,512]{1,0:T(8,128)(2,1)S(1)} collective-permute-done((bf16[144,512]{1,0:T(8,128)(2,1)S(1)}, bf16[144,512]{1,0:T(8,128)(2,1)S(1)}, u32[]{:S(2)}, u32[]{:S(2)}) %collective-permute-start.1) | collective-permute-done | bytes 147488 | tf_op jit(solution)/shard_map/ppermute | solution.py:190
  18.4 0.0 collective-permute-start.4
  18.4 0.0 collective-permute-done.2.refs_3_
  18.4 1.6 %collective-permute-start.9 = (bf16[144,512]{1,0:T(8,128)(2,1)S(1)}, bf16[144,512]{1,0:T(8,128)(2,1)S(1)}, u32[]{:S(2)}, u32[]{:S(2)}) collective-permute-start(bf16[144,512]{1,0:T(8,128)(2,1)S(1)} %collective-permute-done.1.refs_2_), channel_id=1, source_target_pairs={{0,2},{1,3},{2,0},{3,1},{4,6},{5,7},{6,4},{7,5},{8,10},{9,11},{10,... | collective-permute-start | bytes 442376 | tf_op jit(solution)/shard_map/ppermute | solution.py:187
  20.0 0.0 collective-permute-done.7.refs_8_
  20.0 0.2 collective-permute-start.5
  20.1 0.0 collective-permute-done.3.refs_4_
  20.1 0.5 collective-permute-start.10
  20.7 0.7 compare_select_fusion
  21.4 0.2 copy.12
  21.6 0.7 reshape.20.up_fac
  22.3 0.0 collective-permute-done.8.refs_9_
  22.3 0.1 collective-permute-start.6
  22.4 2.8 %collective-permute-done.9.refs_10_ = bf16[144,512]{1,0:T(8,128)(2,1)S(1)} collective-permute-done((bf16[144,512]{1,0:T(8,128)(2,1)S(1)}, bf16[144,512]{1,0:T(8,128)(2,1)S(1)}, u32[]{:S(2)}, u32[]{:S(2)}) %collective-permute-start.9) | collective-permute-done | bytes 147488 | tf_op jit(solution)/shard_map/ppermute | solution.py:187
  25.2 0.0 collective-permute-start.11
  25.2 2.6 %collective-permute-done.10.refs_11_ = bf16[144,512]{1,0:T(8,128)(2,1)S(1)} collective-permute-done((bf16[144,512]{1,0:T(8,128)(2,1)S(1)}, bf16[144,512]{1,0:T(8,128)(2,1)S(1)}, u32[]{:S(2)}, u32[]{:S(2)}) %collective-permute-start.10) | collective-permute-done | bytes 147488 | tf_op jit(solution)/shard_map/ppermute | solution.py:187
  27.8 0.5 collective-permute-start.13
  28.3 0.1 collective-permute-start.14
  28.4 0.7 compare_select_fusion.2
  29.2 0.1 reshape.18.down_fac
  29.3 0.6 stack.23.place_ref
  29.9 0.0 collective-permute-done.12.refs_13_
  29.9 0.0 collective-permute-done.14.refs_15_
  30.0 0.5 copy-done.21
  30.5 0.0 copy-done.22
  30.6 0.1 copy-done.23
  30.6 0.1 copy-done.24
  30.7 0.7 copy-done.25
  31.3 5.8 %copy-done = bf16[16,2048,256]{2,1,0:T(8,128)(2,1)S(1)} copy-done((bf16[16,2048,256]{2,1,0:T(8,128)(2,1)S(1)}, bf16[16,2048,256]{2,1,0:T(8,128)(2,1)}, u32[]{:S(2)}) %copy-start) | copy-done | bytes 16777240
  37.1 5.8 %copy-done.1 = bf16[16,2048,256]{2,1,0:T(8,128)(2,1)S(1)} copy-done((bf16[16,2048,256]{2,1,0:T(8,128)(2,1)S(1)}, bf16[16,2048,256]{2,1,0:T(8,128)(2,1)}, u32[]{:S(2)}) %copy-start.1) | copy-done | bytes 16777240
  42.9 13.3 %up.1 = (bf16[16,96,256]{2,1,0:T(8,128)(2,1)}, bf16[2,256,768]{2,1,0:T(8,128)(2,1)}) custom-call(s32[5]{0:T(128)} %stack.23.place_ref, f32[512]{0:T(512)} %reshape.19.gate_fac, f32[512]{0:T(512)} %reshape.20.up_fac, bf16[144,512]{1,0:T(8,128)(2,1)} %copy-done.5, bf16[144,512]{1,0:T(8,128)(2,1)} %copy-done.11, bf16[144,512]{1,0:T(8,128)(2,1)} %copy-done.12, ...), custom_call_target="tpu_custom_call" | custom-call | tf_op jit(solution)/shard_map/up/pallas_call | solution.py:206
  56.2 0.0 copy-start.2
  56.2 5.8 %copy-done.2 = bf16[16,256,2048]{2,1,0:T(8,128)(2,1)S(1)} copy-done((bf16[16,256,2048]{2,1,0:T(8,128)(2,1)S(1)}, bf16[16,256,2048]{2,1,0:T(8,128)(2,1)}, u32[]{:S(2)}) %copy-start.2) | copy-done | bytes 16777240
  62.0 1.1 %copy-done.3 = bf16[16,96,256]{2,1,0:T(8,128)(2,1)S(1)} copy-done((bf16[16,96,256]{2,1,0:T(8,128)(2,1)S(1)}, bf16[16,96,256]{2,1,0:T(8,128)(2,1)}, u32[]{:S(2)}) %copy-start.3) | copy-done | bytes 786456
  63.1 1.1 %copy-done.4 = bf16[2,256,768]{2,1,0:T(8,128)(2,1)S(1)} copy-done((bf16[2,256,768]{2,1,0:T(8,128)(2,1)S(1)}, bf16[2,256,768]{2,1,0:T(8,128)(2,1)}, u32[]{:S(2)}) %copy-start.4) | copy-done | bytes 786456
  64.2 15.2 %down3210.1 = (bf16[512,512]{1,0:T(8,128)(2,1)S(1)}, bf16[512,512]{1,0:T(8,128)(2,1)S(1)}, bf16[512,512]{1,0:T(8,128)(2,1)S(1)}, bf16[512,512]{1,0:T(8,128)(2,1)S(1)}) custom-call(s32[5]{0:T(128)S(1)} %copy-done.8, f32[512]{0:T(512)S(1)} %reshape.18.down_fac, bf16[16,96,256]{2,1,0:T(8,128)(2,1)S(1)} %copy-done.3, bf16[2,256,768]{2,1,0:T(8,128)(2,1)S(1)} %copy-done.4, ...), custom_call_target="tpu_custom_call" | custom-call | tf_op jit(solution)/shard_map/down3210/pallas_call | solution.py:224
  79.5 0.5 collective-permute-start.16
  79.9 0.1 collective-permute-start.15
  80.0 1.4 %collective-permute-done.16 = bf16[512,512]{1,0:T(8,128)(2,1)S(1)} collective-permute-done((bf16[512,512]{1,0:T(8,128)(2,1)S(1)}, bf16[512,512]{1,0:T(8,128)(2,1)S(1)}, u32[]{:S(2)}, u32[]{:S(2)}) %collective-permute-start.16) | collective-permute-done | bytes 524320 | tf_op jit(solution)/shard_map/ppermute | solution.py:187
  81.5 0.1 add_convert_fusion.1
  81.6 1.6 %collective-permute-start.17 = (bf16[512,512]{1,0:T(8,128)(2,1)S(1)}, bf16[512,512]{1,0:T(8,128)(2,1)S(1)}, u32[]{:S(2)}, u32[]{:S(2)}) collective-permute-start(bf16[512,512]{1,0:T(8,128)(2,1)S(1)} %add_convert_fusion.1), channel_id=1, source_target_pairs={{0,2},{1,3},{2,0},{3,1},{4,6},{5,7},{6,4},{7,5},{8,10},{9,11},{10,... | collective-permute-start | bytes 1572872 | tf_op jit(solution)/shard_map/ppermute | solution.py:187
  83.2 0.0 collective-permute-done.15
  83.2 12.7 %collective-permute-done.17 = bf16[512,512]{1,0:T(8,128)(2,1)S(1)} collective-permute-done((bf16[512,512]{1,0:T(8,128)(2,1)S(1)}, bf16[512,512]{1,0:T(8,128)(2,1)S(1)}, u32[]{:S(2)}, u32[]{:S(2)}) %collective-permute-start.17) | collective-permute-done | bytes 524320 | tf_op jit(solution)/shard_map/ppermute | solution.py:187
  95.9 0.2 add_convert_fusion
  96.1 3.2 %collective-permute-start.18 = (bf16[128,512]{1,0:T(8,128)(2,1)S(1)}, bf16[128,512]{1,0:T(8,128)(2,1)S(1)}, u32[]{:S(2)}, u32[]{:S(2)}) collective-permute-start(bf16[128,512]{1,0:T(8,128)(2,1)S(1)} %get-tuple-element.17), channel_id=1, source_target_pairs={{0,4},{4,8},{8,12},{12,0},{1,5},{5,9},{9,13},{13,1},{2,6},{6,10},{... | collective-permute-start | bytes 393224 | tf_op jit(solution)/shard_map/ppermute | solution.py:190
  99.3 2.1 %collective-permute-start.19 = (bf16[128,512]{1,0:T(8,128)(2,1)S(1)}, bf16[128,512]{1,0:T(8,128)(2,1)S(1)}, u32[]{:S(2)}, u32[]{:S(2)}) collective-permute-start(bf16[128,512]{1,0:T(8,128)(2,1)S(1)} %get-tuple-element.19), channel_id=1, source_target_pairs={{0,8},{4,12},{8,0},{12,4},{1,9},{5,13},{9,1},{13,5},{2,10},{6,14},... | collective-permute-start | bytes 393224 | tf_op jit(solution)/shard_map/ppermute | solution.py:190
  101.4 1.5 %collective-permute-start.20 = (bf16[128,512]{1,0:T(8,128)(2,1)S(1)}, bf16[128,512]{1,0:T(8,128)(2,1)S(1)}, u32[]{:S(2)}, u32[]{:S(2)}) collective-permute-start(bf16[128,512]{1,0:T(8,128)(2,1)S(1)} %get-tuple-element.18), channel_id=1, source_target_pairs={{0,12},{4,0},{8,4},{12,8},{1,13},{5,1},{9,5},{13,9},{2,14},{6,2},{... | collective-permute-start | bytes 393224 | tf_op jit(solution)/shard_map/ppermute | solution.py:190
  102.9 2.4 %collective-permute-done.18 = bf16[128,512]{1,0:T(8,128)(2,1)S(1)} collective-permute-done((bf16[128,512]{1,0:T(8,128)(2,1)S(1)}, bf16[128,512]{1,0:T(8,128)(2,1)S(1)}, u32[]{:S(2)}, u32[]{:S(2)}) %collective-permute-start.18) | collective-permute-done | bytes 131104 | tf_op jit(solution)/shard_map/ppermute | solution.py:190
  105.3 4.4 %collective-permute-done.19 = bf16[128,512]{1,0:T(8,128)(2,1)S(1)} collective-permute-done((bf16[128,512]{1,0:T(8,128)(2,1)S(1)}, bf16[128,512]{1,0:T(8,128)(2,1)S(1)}, u32[]{:S(2)}, u32[]{:S(2)}) %collective-permute-start.19) | collective-permute-done | bytes 131104 | tf_op jit(solution)/shard_map/ppermute | solution.py:190
  109.8 0.7 add_convert_fusion.3
  (47 shorter events, 0.1 us)
Async XLA Ops:
  0.7 0.9 copy-start.6
  1.6 0.7 copy-start.9
  2.3 0.7 copy-start.10
  3.0 26.9 %copy-start.5 = (bf16[144,512]{1,0:T(8,128)(2,1)}, bf16[144,512]{1,0:T(8,128)(2,1)S(1)}, u32[]{:S(2)}) copy-start(bf16[144,512]{1,0:T(8,128)(2,1)S(1)} %pack.1.refs_0_) | copy-start | bytes 442372
  3.0 10.2 %collective-permute-start = (bf16[144,512]{1,0:T(8,128)(2,1)S(1)}, bf16[144,512]{1,0:T(8,128)(2,1)S(1)}, u32[]{:S(2)}, u32[]{:S(2)}) collective-permute-start(bf16[144,512]{1,0:T(8,128)(2,1)S(1)} %pack.1.refs_0_), channel_id=1, source_target_pairs={{0,4},{4,8},{8,12},{12,0},{1,5},{5,9},{9,13},{13,1},{2,6},{6,10},{... | collective-permute-start | bytes 442376 | tf_op jit(solution)/shard_map/ppermute | solution.py:190
  6.1 12.3 %collective-permute-start.1 = (bf16[144,512]{1,0:T(8,128)(2,1)S(1)}, bf16[144,512]{1,0:T(8,128)(2,1)S(1)}, u32[]{:S(2)}, u32[]{:S(2)}) collective-permute-start(bf16[144,512]{1,0:T(8,128)(2,1)S(1)} %pack.1.refs_0_), channel_id=1, source_target_pairs={{0,8},{4,12},{8,0},{12,4},{1,9},{5,13},{9,1},{13,5},{2,10},{6,14},... | collective-permute-start | bytes 442376 | tf_op jit(solution)/shard_map/ppermute | solution.py:190
  8.7 9.7 %collective-permute-start.2 = (bf16[144,512]{1,0:T(8,128)(2,1)S(1)}, bf16[144,512]{1,0:T(8,128)(2,1)S(1)}, u32[]{:S(2)}, u32[]{:S(2)}) collective-permute-start(bf16[144,512]{1,0:T(8,128)(2,1)S(1)} %pack.1.refs_0_), channel_id=1, source_target_pairs={{0,12},{4,0},{8,4},{12,8},{1,13},{5,1},{9,5},{13,9},{2,14},{6,2},{... | collective-permute-start | bytes 442376 | tf_op jit(solution)/shard_map/ppermute | solution.py:190
  10.0 9.9 %collective-permute-start.7 = (bf16[144,512]{1,0:T(8,128)(2,1)S(1)}, bf16[144,512]{1,0:T(8,128)(2,1)S(1)}, u32[]{:S(2)}, u32[]{:S(2)}) collective-permute-start(bf16[144,512]{1,0:T(8,128)(2,1)S(1)} %pack.1.refs_0_), channel_id=1, source_target_pairs={{0,2},{1,3},{2,0},{3,1},{4,6},{5,7},{6,4},{7,5},{8,10},{9,11},{10,... | collective-permute-start | bytes 442376 | tf_op jit(solution)/shard_map/ppermute | solution.py:187
  11.5 8.6 %collective-permute-start.3 = (bf16[144,512]{1,0:T(8,128)(2,1)S(1)}, bf16[144,512]{1,0:T(8,128)(2,1)S(1)}, u32[]{:S(2)}, u32[]{:S(2)}) collective-permute-start(bf16[144,512]{1,0:T(8,128)(2,1)S(1)} %pack.1.refs_0_), channel_id=1, source_target_pairs={{0,1},{1,0},{2,3},{3,2},{4,5},{5,4},{6,7},{7,6},{8,9},{9,8},{10,11... | collective-permute-start | bytes 442376 | tf_op jit(solution)/shard_map/ppermute | solution.py:187
  13.2 16.8 %copy-start.11 = (bf16[144,512]{1,0:T(8,128)(2,1)}, bf16[144,512]{1,0:T(8,128)(2,1)S(1)}, u32[]{:S(2)}) copy-start(bf16[144,512]{1,0:T(8,128)(2,1)S(1)} %collective-permute-done.refs_1_) | copy-start | bytes 442372
  13.2 9.1 %collective-permute-start.8 = (bf16[144,512]{1,0:T(8,128)(2,1)S(1)}, bf16[144,512]{1,0:T(8,128)(2,1)S(1)}, u32[]{:S(2)}, u32[]{:S(2)}) collective-permute-start(bf16[144,512]{1,0:T(8,128)(2,1)S(1)} %collective-permute-done.refs_1_), channel_id=1, source_target_pairs={{0,2},{1,3},{2,0},{3,1},{4,6},{5,7},{6,4},{7,5},{8,10},{9,11},{10,... | collective-permute-start | bytes 442376 | tf_op jit(solution)/shard_map/ppermute | solution.py:187
  18.4 11.6 %copy-start.12 = (bf16[144,512]{1,0:T(8,128)(2,1)}, bf16[144,512]{1,0:T(8,128)(2,1)S(1)}, u32[]{:S(2)}) copy-start(bf16[144,512]{1,0:T(8,128)(2,1)S(1)} %collective-permute-done.1.refs_2_) | copy-start | bytes 442372
  18.4 9.4 %collective-permute-start.4 = (bf16[144,512]{1,0:T(8,128)(2,1)S(1)}, bf16[144,512]{1,0:T(8,128)(2,1)S(1)}, u32[]{:S(2)}, u32[]{:S(2)}) collective-permute-start(bf16[144,512]{1,0:T(8,128)(2,1)S(1)} %collective-permute-done.refs_1_), channel_id=1, source_target_pairs={{0,1},{1,0},{2,3},{3,2},{4,5},{5,4},{6,7},{7,6},{8,9},{9,8},{10,11... | collective-permute-start | bytes 442376 | tf_op jit(solution)/shard_map/ppermute | solution.py:187
  18.4 11.6 %copy-start.13 = (bf16[144,512]{1,0:T(8,128)(2,1)}, bf16[144,512]{1,0:T(8,128)(2,1)S(1)}, u32[]{:S(2)}) copy-start(bf16[144,512]{1,0:T(8,128)(2,1)S(1)} %collective-permute-done.2.refs_3_) | copy-start | bytes 442372
  18.4 6.8 %collective-permute-start.9 = (bf16[144,512]{1,0:T(8,128)(2,1)S(1)}, bf16[144,512]{1,0:T(8,128)(2,1)S(1)}, u32[]{:S(2)}, u32[]{:S(2)}) collective-permute-start(bf16[144,512]{1,0:T(8,128)(2,1)S(1)} %collective-permute-done.1.refs_2_), channel_id=1, source_target_pairs={{0,2},{1,3},{2,0},{3,1},{4,6},{5,7},{6,4},{7,5},{8,10},{9,11},{10,... | collective-permute-start | bytes 442376 | tf_op jit(solution)/shard_map/ppermute | solution.py:187
  20.0 10.0 %copy-start.14 = (bf16[144,512]{1,0:T(8,128)(2,1)}, bf16[144,512]{1,0:T(8,128)(2,1)S(1)}, u32[]{:S(2)}) copy-start(bf16[144,512]{1,0:T(8,128)(2,1)S(1)} %collective-permute-done.7.refs_8_) | copy-start | bytes 442372
  20.0 8.4 %collective-permute-start.5 = (bf16[144,512]{1,0:T(8,128)(2,1)S(1)}, bf16[144,512]{1,0:T(8,128)(2,1)S(1)}, u32[]{:S(2)}, u32[]{:S(2)}) collective-permute-start(bf16[144,512]{1,0:T(8,128)(2,1)S(1)} %collective-permute-done.1.refs_2_), channel_id=1, source_target_pairs={{0,1},{1,0},{2,3},{3,2},{4,5},{5,4},{6,7},{7,6},{8,9},{9,8},{10,11... | collective-permute-start | bytes 442376 | tf_op jit(solution)/shard_map/ppermute | solution.py:187
  20.1 9.9 %copy-start.15 = (bf16[144,512]{1,0:T(8,128)(2,1)}, bf16[144,512]{1,0:T(8,128)(2,1)S(1)}, u32[]{:S(2)}) copy-start(bf16[144,512]{1,0:T(8,128)(2,1)S(1)} %collective-permute-done.3.refs_4_) | copy-start | bytes 442372
  20.1 7.7 %collective-permute-start.10 = (bf16[144,512]{1,0:T(8,128)(2,1)S(1)}, bf16[144,512]{1,0:T(8,128)(2,1)S(1)}, u32[]{:S(2)}, u32[]{:S(2)}) collective-permute-start(bf16[144,512]{1,0:T(8,128)(2,1)S(1)} %collective-permute-done.2.refs_3_), channel_id=1, source_target_pairs={{0,2},{1,3},{2,0},{3,1},{4,6},{5,7},{6,4},{7,5},{8,10},{9,11},{10,... | collective-permute-start | bytes 442376 | tf_op jit(solution)/shard_map/ppermute | solution.py:187
  22.3 7.7 %copy-start.16 = (bf16[144,512]{1,0:T(8,128)(2,1)}, bf16[144,512]{1,0:T(8,128)(2,1)S(1)}, u32[]{:S(2)}) copy-start(bf16[144,512]{1,0:T(8,128)(2,1)S(1)} %collective-permute-done.8.refs_9_) | copy-start | bytes 442372
  22.3 7.5 %collective-permute-start.6 = (bf16[144,512]{1,0:T(8,128)(2,1)S(1)}, bf16[144,512]{1,0:T(8,128)(2,1)S(1)}, u32[]{:S(2)}, u32[]{:S(2)}) collective-permute-start(bf16[144,512]{1,0:T(8,128)(2,1)S(1)} %collective-permute-done.2.refs_3_), channel_id=1, source_target_pairs={{0,1},{1,0},{2,3},{3,2},{4,5},{5,4},{6,7},{7,6},{8,9},{9,8},{10,11... | collective-permute-start | bytes 442376 | tf_op jit(solution)/shard_map/ppermute | solution.py:187
  25.2 4.8 %copy-start.18 = (bf16[144,512]{1,0:T(8,128)(2,1)}, bf16[144,512]{1,0:T(8,128)(2,1)S(1)}, u32[]{:S(2)}) copy-start(bf16[144,512]{1,0:T(8,128)(2,1)S(1)} %collective-permute-done.9.refs_10_) | copy-start | bytes 442372
  25.2 4.7 %collective-permute-start.11 = (bf16[144,512]{1,0:T(8,128)(2,1)S(1)}, bf16[144,512]{1,0:T(8,128)(2,1)S(1)}, u32[]{:S(2)}, u32[]{:S(2)}) collective-permute-start(bf16[144,512]{1,0:T(8,128)(2,1)S(1)} %collective-permute-done.7.refs_8_), channel_id=1, source_target_pairs={{0,1},{1,0},{2,3},{3,2},{4,5},{5,4},{6,7},{7,6},{8,9},{9,8},{10,11... | collective-permute-start | bytes 442376 | tf_op jit(solution)/shard_map/ppermute | solution.py:187
  27.8 2.2 %copy-start.20 = (bf16[144,512]{1,0:T(8,128)(2,1)}, bf16[144,512]{1,0:T(8,128)(2,1)S(1)}, u32[]{:S(2)}) copy-start(bf16[144,512]{1,0:T(8,128)(2,1)S(1)} %collective-permute-done.10.refs_11_) | copy-start | bytes 442372
  27.8 2.1 %collective-permute-start.12 = (bf16[144,512]{1,0:T(8,128)(2,1)S(1)}, bf16[144,512]{1,0:T(8,128)(2,1)S(1)}, u32[]{:S(2)}, u32[]{:S(2)}) collective-permute-start(bf16[144,512]{1,0:T(8,128)(2,1)S(1)} %collective-permute-done.8.refs_9_), channel_id=1, source_target_pairs={{0,1},{1,0},{2,3},{3,2},{4,5},{5,4},{6,7},{7,6},{8,9},{9,8},{10,11... | collective-permute-start | bytes 442376 | tf_op jit(solution)/shard_map/ppermute | solution.py:187
  27.8 2.2 %copy-start.17 = (bf16[144,512]{1,0:T(8,128)(2,1)}, bf16[144,512]{1,0:T(8,128)(2,1)S(1)}, u32[]{:S(2)}) copy-start(bf16[144,512]{1,0:T(8,128)(2,1)S(1)} %collective-permute-done.4.refs_5_) | copy-start | bytes 442372
  27.8 2.1 %collective-permute-start.13 = (bf16[144,512]{1,0:T(8,128)(2,1)S(1)}, bf16[144,512]{1,0:T(8,128)(2,1)S(1)}, u32[]{:S(2)}, u32[]{:S(2)}) collective-permute-start(bf16[144,512]{1,0:T(8,128)(2,1)S(1)} %collective-permute-done.9.refs_10_), channel_id=1, source_target_pairs={{0,1},{1,0},{2,3},{3,2},{4,5},{5,4},{6,7},{7,6},{8,9},{9,8},{10,11... | collective-permute-start | bytes 442376 | tf_op jit(solution)/shard_map/ppermute | solution.py:187
  28.3 1.7 %copy-start.19 = (bf16[144,512]{1,0:T(8,128)(2,1)}, bf16[144,512]{1,0:T(8,128)(2,1)S(1)}, u32[]{:S(2)}) copy-start(bf16[144,512]{1,0:T(8,128)(2,1)S(1)} %collective-permute-done.5.refs_6_) | copy-start | bytes 442372
  28.3 1.6 %collective-permute-start.14 = (bf16[144,512]{1,0:T(8,128)(2,1)S(1)}, bf16[144,512]{1,0:T(8,128)(2,1)S(1)}, u32[]{:S(2)}, u32[]{:S(2)}) collective-permute-start(bf16[144,512]{1,0:T(8,128)(2,1)S(1)} %collective-permute-done.10.refs_11_), channel_id=1, source_target_pairs={{0,1},{1,0},{2,3},{3,2},{4,5},{5,4},{6,7},{7,6},{8,9},{9,8},{10,11... | collective-permute-start | bytes 442376 | tf_op jit(solution)/shard_map/ppermute | solution.py:187
  29.9 0.7 copy-start.21
  29.9 0.7 copy-start.22
  29.9 0.7 copy-start.23
  29.9 0.8 copy-start.24
  30.7 0.7 copy-start.25
  31.3 5.8 %copy-start = (bf16[16,2048,256]{2,1,0:T(8,128)(2,1)S(1)}, bf16[16,2048,256]{2,1,0:T(8,128)(2,1)}, u32[]{:S(2)}) copy-start(bf16[16,2048,256]{2,1,0:T(8,128)(2,1)} %refs_16_.1) | copy-start | bytes 50331652
  37.1 5.8 %copy-start.1 = (bf16[16,2048,256]{2,1,0:T(8,128)(2,1)S(1)}, bf16[16,2048,256]{2,1,0:T(8,128)(2,1)}, u32[]{:S(2)}) copy-start(bf16[16,2048,256]{2,1,0:T(8,128)(2,1)} %refs_17_.1) | copy-start | bytes 50331652
  42.9 13.3 %copy-start.8 = (s32[5]{0:T(128)S(1)}, s32[5]{0:T(128)}, u32[]{:S(2)}) copy-start(s32[5]{0:T(128)} %stack.23.place_ref) | copy-start | bytes 64
  42.9 66.9 %copy-start.7 = (bf16[128,512]{1,0:T(8,128)(2,1)S(1)}, bf16[128,512]{1,0:T(8,128)(2,1)}, u32[]{:S(2)}) copy-start(bf16[128,512]{1,0:T(8,128)(2,1)} %rows_ref.1) | copy-start | bytes 393220
  56.2 5.8 %copy-start.2 = (bf16[16,256,2048]{2,1,0:T(8,128)(2,1)S(1)}, bf16[16,256,2048]{2,1,0:T(8,128)(2,1)}, u32[]{:S(2)}) copy-start(bf16[16,256,2048]{2,1,0:T(8,128)(2,1)} %down_ref.1) | copy-start | bytes 50331652
  62.0 1.1 %copy-start.3 = (bf16[16,96,256]{2,1,0:T(8,128)(2,1)S(1)}, bf16[16,96,256]{2,1,0:T(8,128)(2,1)}, u32[]{:S(2)}) copy-start(bf16[16,96,256]{2,1,0:T(8,128)(2,1)} %get-tuple-element.11.act_ref) | copy-start | bytes 2359300
  63.1 1.1 %copy-start.4 = (bf16[2,256,768]{2,1,0:T(8,128)(2,1)S(1)}, bf16[2,256,768]{2,1,0:T(8,128)(2,1)}, u32[]{:S(2)}) copy-start(bf16[2,256,768]{2,1,0:T(8,128)(2,1)} %get-tuple-element.12.comb_ref) | copy-start | bytes 2359300
  79.5 2.0 %collective-permute-start.16 = (bf16[512,512]{1,0:T(8,128)(2,1)S(1)}, bf16[512,512]{1,0:T(8,128)(2,1)S(1)}, u32[]{:S(2)}, u32[]{:S(2)}) collective-permute-start(bf16[512,512]{1,0:T(8,128)(2,1)S(1)} %get-tuple-element.16), channel_id=1, source_target_pairs={{0,1},{1,0},{2,3},{3,2},{4,5},{5,4},{6,7},{7,6},{8,9},{9,8},{10,11... | collective-permute-start | bytes 1572872 | tf_op jit(solution)/shard_map/ppermute | solution.py:187
  79.9 3.2 %collective-permute-start.15 = (bf16[512,512]{1,0:T(8,128)(2,1)S(1)}, bf16[512,512]{1,0:T(8,128)(2,1)S(1)}, u32[]{:S(2)}, u32[]{:S(2)}) collective-permute-start(bf16[512,512]{1,0:T(8,128)(2,1)S(1)} %get-tuple-element.14), channel_id=1, source_target_pairs={{0,1},{1,0},{2,3},{3,2},{4,5},{5,4},{6,7},{7,6},{8,9},{9,8},{10,11... | collective-permute-start | bytes 1572872 | tf_op jit(solution)/shard_map/ppermute | solution.py:187
  81.6 14.3 %collective-permute-start.17 = (bf16[512,512]{1,0:T(8,128)(2,1)S(1)}, bf16[512,512]{1,0:T(8,128)(2,1)S(1)}, u32[]{:S(2)}, u32[]{:S(2)}) collective-permute-start(bf16[512,512]{1,0:T(8,128)(2,1)S(1)} %add_convert_fusion.1), channel_id=1, source_target_pairs={{0,2},{1,3},{2,0},{3,1},{4,6},{5,7},{6,4},{7,5},{8,10},{9,11},{10,... | collective-permute-start | bytes 1572872 | tf_op jit(solution)/shard_map/ppermute | solution.py:187
  96.1 9.2 %collective-permute-start.18 = (bf16[128,512]{1,0:T(8,128)(2,1)S(1)}, bf16[128,512]{1,0:T(8,128)(2,1)S(1)}, u32[]{:S(2)}, u32[]{:S(2)}) collective-permute-start(bf16[128,512]{1,0:T(8,128)(2,1)S(1)} %get-tuple-element.17), channel_id=1, source_target_pairs={{0,4},{4,8},{8,12},{12,0},{1,5},{5,9},{9,13},{13,1},{2,6},{6,10},{... | collective-permute-start | bytes 393224 | tf_op jit(solution)/shard_map/ppermute | solution.py:190
  99.3 10.4 %collective-permute-start.19 = (bf16[128,512]{1,0:T(8,128)(2,1)S(1)}, bf16[128,512]{1,0:T(8,128)(2,1)S(1)}, u32[]{:S(2)}, u32[]{:S(2)}) collective-permute-start(bf16[128,512]{1,0:T(8,128)(2,1)S(1)} %get-tuple-element.19), channel_id=1, source_target_pairs={{0,8},{4,12},{8,0},{12,4},{1,9},{5,13},{9,1},{13,5},{2,10},{6,14},... | collective-permute-start | bytes 393224 | tf_op jit(solution)/shard_map/ppermute | solution.py:190
  101.4 8.3 %collective-permute-start.20 = (bf16[128,512]{1,0:T(8,128)(2,1)S(1)}, bf16[128,512]{1,0:T(8,128)(2,1)S(1)}, u32[]{:S(2)}, u32[]{:S(2)}) collective-permute-start(bf16[128,512]{1,0:T(8,128)(2,1)S(1)} %get-tuple-element.18), channel_id=1, source_target_pairs={{0,12},{4,0},{8,4},{12,8},{1,13},{5,1},{9,5},{13,9},{2,14},{6,2},{... | collective-permute-start | bytes 393224 | tf_op jit(solution)/shard_map/ppermute | solution.py:190

commit v2 on v1

v2 whole, which is shorter than its diff:
```python
import functools

import jax
import jax.numpy as jnp
from jax import lax
from jax.experimental import pallas as pl
from jax.experimental.pallas import tpu as pltpu
from jax.sharding import PartitionSpec as P

QB = 128
CAP = 24
EXTRA = 16
EPSILON = 1e-06
MIB = 1 << 20
UP_VMEM = 10
DOWN_VMEM = 4
UNROLL = 4
GROUP = 4


def power_two(exponent):
    magnitude = jnp.left_shift(jnp.ones_like(exponent), jnp.abs(exponent)).astype(jnp.float32)
    return jnp.where(exponent >= 0, magnitude, 1.0 / magnitude)


def pack_kernel(rows_hbm, gain_hbm, ids_hbm, scores_hbm, *refs):
    out_ref, ids_ref, scores_ref, gain_ref, sems = refs[-5:]
    tokens, width = rows_hbm.shape
    top = ids_ref.shape[0]
    moves = [
        pltpu.make_async_copy(ids_hbm, ids_ref, sems.at[0]),
        pltpu.make_async_copy(scores_hbm, scores_ref, sems.at[1]),
        pltpu.make_async_copy(rows_hbm, out_ref.at[pl.ds(0, tokens), :], sems.at[2]),
        pltpu.make_async_copy(gain_hbm, gain_ref, sems.at[3]),
    ]
    for move in moves:
        move.start()
    moves[3].wait()
    gain = jnp.broadcast_to(gain_ref[...].astype(jnp.float32)[None, :], (EXTRA - top, width))
    moves[0].wait()
    moves[1].wait()
    raised = jnp.exp(scores_ref[...])
    weights = raised / jnp.sum(raised, axis=0, keepdims=True)
    routes = jnp.concatenate((ids_ref[...].astype(jnp.float32), weights), axis=1)
    if width > 2 * tokens:
        routes = jnp.concatenate((routes, jnp.zeros((top, width - 2 * tokens), jnp.float32)), axis=1)
    out_ref[tokens:, :] = jnp.concatenate((routes, gain), axis=0).astype(jnp.bfloat16)
    moves[2].wait()


def scaled(block, exponents):
    parts = []
    for i, value in enumerate(exponents):
        piece = block[i * QB : (i + 1) * QB]
        by = jnp.left_shift(1, value + 15).astype(jnp.float32) * (1.0 / 32768.0)
        by = jnp.full((16, QB), by, jnp.float32).astype(jnp.bfloat16)
        parts.append((piece.reshape(QB // 16, 16, QB) * by[None]).reshape(QB, QB))
    return parts[0] if len(parts) == 1 else jnp.concatenate(parts, axis=0)


def head_of(f, split):
    return lax.axis_index("head") ^ f if split else f


def up_kernel(n_head, n_block, split, group, gate_exp, up_exp, *refs):
    n_piece = n_head * n_block if split else 1
    pieces = refs[:n_piece]
    gate_ref, up_ref, act_ref, comb_ref, normed, taken, slots = refs[n_piece:]

    def piece(f, j):
        return pieces[f * n_block + j] if split else pieces[0].at[f, j]

    experts, features, hidden = gate_ref.shape
    width = features // n_head
    tokens = normed.shape[0] // n_block
    pair = 2 * tokens
    slot = 2 * CAP
    cols = hidden // QB
    top = 8
    n_pair = n_block // 2
    for j in range(n_block):
        total = jnp.zeros((tokens, 1), jnp.float32)
        for f in range(n_head):
            value = piece(f, j)[:tokens, :].astype(jnp.float32)
            total = total + jnp.sum(value * value, axis=1, keepdims=True)
        scale = lax.rsqrt(total / features + EPSILON)
        for f in range(n_head):
            value = piece(f, j)[:tokens, :].astype(jnp.float32)
            gain = piece(f, j)[tokens + top : tokens + top + 8, :].astype(jnp.float32)[0:1, :]
            normed[pl.ds(j * tokens, tokens), pl.ds(f * width, width)] = (
                value * scale * gain
            ).astype(jnp.bfloat16)
    first = lax.axis_index("expert") * experts
    row = lax.broadcasted_iota(jnp.int32, (pair, pair), 0)
    col = lax.broadcasted_iota(jnp.int32, (pair, pair), 1)
    before = ((row < col) & ((row >= tokens) | (col < tokens))).astype(jnp.bfloat16)
    expert = (lax.broadcasted_iota(jnp.int32, (experts, pair), 0) + first).astype(jnp.float32)
    second = lax.broadcasted_iota(jnp.int32, (experts, pair), 1) >= tokens
    slot_no = lax.broadcasted_iota(jnp.int32, (slot, pair), 0).astype(jnp.float32)
    for p in range(n_block // 2):
        lists = [piece(0, 2 * p + i)[tokens : tokens + top, : 2 * tokens].astype(jnp.float32) for i in range(2)]
        ids = jnp.concatenate([x[:, :tokens] for x in lists], axis=1)
        weights = jnp.concatenate([x[:, tokens:] for x in lists], axis=1)
        named = jnp.zeros((experts, pair), jnp.float32)
        weight = jnp.zeros((experts, pair), jnp.float32)
        for k in range(top):
            same = ids[k : k + 1, :] == expert
            named = jnp.where(same, 1.0, named)
            weight = jnp.where(same, weights[k : k + 1, :], weight)
        rank = jnp.dot(named.astype(jnp.bfloat16), before, preferred_element_type=jnp.float32)
        target = jnp.where(named > 0, rank + jnp.where(second, float(CAP), 0.0), -1.0)
        back = []
        for e in range(experts):
            here = target[e : e + 1, :] == slot_no
            taken[p, pl.ds(e * slot, slot), :] = jnp.where(here, 1.0, 0.0).astype(jnp.bfloat16)
            back.append(jnp.where(here, weight[e : e + 1, :], 0.0))
        comb_ref[p] = jnp.transpose(jnp.concatenate(back, axis=0)).astype(jnp.bfloat16)

    per_piece = width // QB
    step = min(features, 512)

    def one_group(g, carry):
        for p in range(n_pair):
            chosen = taken[p, pl.ds(pl.multiple_of(g * (group * slot), group * slot), group * slot), :]
            for n in range(features // step):
                rows = jnp.dot(
                    chosen,
                    normed[pl.ds(p * pair, pair), pl.ds(n * step, step)],
                    preferred_element_type=jnp.float32,
                ).astype(jnp.bfloat16)
                slots[:, pl.ds(p * slot, slot), pl.ds(n * step, step)] = rows.reshape(group, slot, step)
        for i in range(group):
            e = g * group + i
            outs = []
            for ref, exp in ((gate_ref, gate_exp), (up_ref, up_exp)):
                acc = None
                for f in range(n_head):
                    at = head_of(f, split)
                    start = pl.multiple_of(at * width, width)
                    left = slots[i, :, pl.ds(f * width, width)]
                    block = ref[e, pl.ds(start, width), :]
                    right = [
                        scaled(
                            block[:, n * QB : (n + 1) * QB],
                            [exp[e, n, at * per_piece + k] for k in range(per_piece)],
                        )
                        for n in range(cols)
                    ]
                    right = right[0] if cols == 1 else jnp.concatenate(right, axis=1)
                    term = jnp.dot(left, right, preferred_element_type=jnp.float32)
                    acc = term if acc is None else acc + term
                outs.append(acc)
            gate_out, up_out = outs
            act = gate_out / (1.0 + jnp.exp(-gate_out)) * up_out
            act_ref[e] = act.astype(jnp.bfloat16)
        return carry

    lax.fori_loop(0, experts // group, one_group, 0)


def down_kernel(f, n_head, split, down_exp, act_ref, comb_ref, down_ref, *refs):
    outs, partial = refs[:-1], refs[-1]
    experts, hidden, features = down_ref.shape
    width = features // n_head
    n_pair, pair, _ = comb_ref.shape
    slot = 2 * CAP
    per_piece = width // QB
    at = head_of(f, split)
    start = pl.multiple_of(at * width, width)

    def one_expert(e, carry):
        block = down_ref[e, :, pl.ds(start, width)]
        right = jnp.concatenate(
            [
                scaled(
                    block[:, n * QB : (n + 1) * QB],
                    [down_exp[e, i, at * per_piece + n] for i in range(hidden // QB)],
                )
                for n in range(per_piece)
            ],
            axis=1,
        )
        value = jnp.dot(act_ref[e], right, preferred_element_type=jnp.float32).astype(jnp.bfloat16)
        for p in range(n_pair):
            partial[p, pl.ds(pl.multiple_of(e * slot, slot), slot), :] = value[p * slot : (p + 1) * slot]
        return carry

    lax.fori_loop(0, experts, one_expert, 0, unroll=min(experts, UNROLL))
    for p in range(n_pair):
        value = jnp.dot(comb_ref[p], partial[p], preferred_element_type=jnp.float32).astype(jnp.bfloat16)
        if len(outs) == 1:
            outs[0][pl.ds(p * pair, pair), :] = value
        else:
            outs[2 * p][...] = value[: pair // 2]
            outs[2 * p + 1][...] = value[pair // 2 :]


def on_device(n_expert, n_head, residual_in, norm_gain, expert_ids, route_scores,
              gate_weight, up_weight, down_weight, gate_exp, up_exp, down_exp):
    tokens, width = residual_in.shape
    experts, features, hidden = gate_weight.shape
    split = n_head == 4 and n_expert <= 4
    vmem, smem = pl.BlockSpec(memory_space=pltpu.VMEM), pl.BlockSpec(memory_space=pltpu.SMEM)
    hbm = pl.BlockSpec(memory_space=pltpu.HBM)
    top = expert_ids.shape[1]
    packed = pl.pallas_call(
        pack_kernel,
        out_shape=jax.ShapeDtypeStruct((tokens + EXTRA, width), jnp.bfloat16),
        in_specs=[hbm] * 7,
        out_specs=vmem,
        scratch_shapes=[
            pltpu.VMEM((top, tokens), jnp.int32),
            pltpu.VMEM((top, tokens), jnp.float32),
            pltpu.VMEM((width,), jnp.bfloat16),
            pltpu.SemaphoreType.DMA((4,)),
        ],
        compiler_params=pltpu.CompilerParams(vmem_limit_bytes=MIB),
        name="pack",
    )(HB(residual_in), HB(norm_gain), HB(expert_ids.T), HB(route_scores.T), HB(gate_weight), HB(up_weight), HB(down_weight))

    def swap(value, bit):
        return lax.ppermute(value, "head", [(i, i ^ bit) for i in range(n_head)])

    def shift(value, k):
        return lax.ppermute(value, "expert", [(i, (i + k) % n_expert) for i in range(n_expert)])

    bits = [1 << i for i in range(n_head.bit_length() - 1)]
    if split:
        pieces = {0: [packed] + [shift(packed, k) for k in range(1, n_expert)]}
        for bit in reversed(bits):
            for f in list(pieces):
                pieces[f | bit] = [swap(value, bit) for value in pieces[f]]
        gathered = [value for f in range(n_head) for value in pieces[f]]
    else:
        gathered = [lax.all_gather(lax.all_gather(packed, "expert"), "head")]
    group = min(experts, GROUP)
    gate_exp, up_exp = (jnp.transpose(x, (0, 2, 1)) for x in (gate_exp, up_exp))
    n_pair, pair, slot = n_expert // 2, 2 * tokens, 2 * CAP
    act, comb = pl.pallas_call(
        functools.partial(up_kernel, n_head, n_expert, split, group),
        out_shape=(
            jax.ShapeDtypeStruct((experts, n_pair * slot, hidden), jnp.bfloat16),
            jax.ShapeDtypeStruct((n_pair, pair, experts * slot), jnp.bfloat16),
        ),
        in_specs=[smem] * 2 + [vmem] * (len(gathered) + 2),
        out_specs=(vmem, vmem),
        scratch_shapes=[
            pltpu.VMEM((n_expert * tokens, features), jnp.bfloat16),
            pltpu.VMEM((n_pair, experts * slot, pair), jnp.bfloat16),
            pltpu.VMEM((group, n_pair * slot, features), jnp.bfloat16),
        ],
        compiler_params=pltpu.CompilerParams(vmem_limit_bytes=UP_VMEM * MIB),
        name="up",
    )(gate_exp, up_exp, *gathered, VM(gate_weight), VM(up_weight))

    def down(f, blocks):
        rows = n_expert * tokens // blocks
        return pl.pallas_call(
            functools.partial(down_kernel, f, n_head, split),
            out_shape=[jax.ShapeDtypeStruct((rows, width), jnp.bfloat16)] * blocks,
            in_specs=[smem] + [vmem] * 3,
            out_specs=[vmem] * blocks,
            scratch_shapes=[pltpu.VMEM((n_pair, experts * slot, width), jnp.bfloat16)],
            compiler_params=pltpu.CompilerParams(vmem_limit_bytes=DOWN_VMEM * MIB),
            name="down" + str(f),
        )(down_exp, act, comb, VM(down_weight))

    def add(*terms):
        return functools.reduce(jnp.add, [t.astype(jnp.float32) for t in terms]).astype(jnp.bfloat16)

    def rows_of(value, j):
        return value[j * tokens : (j + 1) * tokens]

    own = residual_in.astype(jnp.float32)
    if split:
        (far,) = down(3, 1)
        near = down(2, n_expert)
        far = swap(far, 1)
        order = list(range(1, n_expert)) + [0]
        crossed = {j: swap(add(near[j], rows_of(far, j)), 2) for j in order}
        (beside,) = down(1, 1)
        mine = down(0, n_expert)
        beside = swap(beside, 1)
        combined = own
        for j in order:
            total = add(mine[j], rows_of(beside, j), crossed[j])
            combined = combined + (shift(total, n_expert - j) if j else total).astype(jnp.float32)
    else:
        parts = jnp.stack([down(f, 1)[0] for f in range(n_head)])
        mine = lax.psum_scatter(parts, "head", scatter_dimension=0)
        mine = mine.reshape(n_expert, tokens, width)
        combined = own + lax.psum_scatter(mine, "expert", scatter_dimension=0).astype(jnp.float32)
    return combined.astype(jnp.bfloat16)


def HB(x):
    return pltpu.with_memory_space_constraint(x, pltpu.HBM)


def VM(x):
    return pltpu.with_memory_space_constraint(x, pltpu.VMEM)


def solution(mesh):
    placed = (
        P(("group", "expert"), "head"),
        P("head"),
        P(("group", "expert"), None),
        P(("group", "expert"), None),
        P("expert", None, "head"),
        P("expert", None, "head"),
        P("expert", "head", None),
        P("expert", None, "head"),
        P("expert", None, "head"),
        P("expert", "head", None),
    )
    return jax.shard_map(
        functools.partial(on_device, mesh.shape["expert"], mesh.shape["head"]),
        mesh=mesh,
        in_specs=placed,
        out_specs=P(("group", "expert"), "head"),
        check_vma=False,
    )
```

time: 112 us -> 75.7 us (0.68); the launches traced: 111 us -> 75.6 us
  local copies, waits for them, and re-layouts: 26.4 us -> 0.05 us
  Pallas kernels: 28.5 us -> 22.9 us
  starting transfers between devices: 21.8 us -> 17.8 us
  waiting for transfers between devices: 30.2 us -> 33.6 us
  other arithmetic: 3.3 us -> 1.07 us
    unnamed x52 -> x20, local copies, waits for them, and re-layouts: 23.2 us -> 0.05 us
    ppermute x6, waiting for transfers between devices: 10.6 us -> 20.9 us  [shift(): lax.ppermute(value, 'expert', [(i, (i + k) % n_expert) for i in range(n_e...]
    ppermute x6, starting transfers between devices: 13.8 us -> 6.77 us  [shift(): lax.ppermute(value, 'expert', [(i, (i + k) % n_expert) for i in range(n_e...]
    ppermute x15 -> x18, waiting for transfers between devices: 19.6 us -> 12.7 us  [swap(): return lax.ppermute(value, 'head', [(i, i ^ bit) for i in range(n_head)])]
    pallas_call x2 -> x5, Pallas kernels: 28.5 us -> 21.8 us  [the longest x4 10.9 us: down(): pl.pallas_call(functools.partial(down_kernel, f, n_head, split), out_shap...]
    ppermute x15 -> x18, starting transfers between devices: 8 us -> 11 us  [swap(): return lax.ppermute(value, 'head', [(i, i ^ bit) for i in range(n_head)])]
    select_n x3 -> x0, other arithmetic: 2.22 us -> none  [power_two(): return jnp.where(exponent >= 0, magnitude, 1.0 / magnitude)]
    reshape x3 -> x0, local copies, waits for them, and re-layouts: 1.54 us -> none  [on_device(): factors = [power_two(x).reshape(-1) for x in (gate_exp, up_exp, down_exp)]]
  transfers between devices with their start and end apart: 21 -> 24, of which waited for: 7 -> 10; matrix products, arithmetic and copies ran while one was open for 4% -> 0% of each run, Pallas kernels for 0% -> 11%
where the time goes in v2:
time: 75.7 us; the launch traced here: 75.6 us
  waiting for transfers between devices  33.6 us (44%)
  Pallas kernels  22.9 us (30%)
  starting transfers between devices  17.8 us (24%)
  other arithmetic  1.07 us (1%)
    ppermute x6, waiting for transfers between devices, shift(): lax.ppermute(value, 'expert', [(i, (i + k) % n_expert) for i in range(n_e...  20.9 us
    ppermute x18, waiting for transfers between devices, swap(): return lax.ppermute(value, 'head', [(i, i ^ bit) for i in range(n_head)])  12.7 us
    ppermute x18, starting transfers between devices, swap(): return lax.ppermute(value, 'head', [(i, i ^ bit) for i in range(n_head)])  11 us
    pallas_call x4, Pallas kernels, down(): pl.pallas_call(functools.partial(down_kernel, f, n_head, split), out_shap...  10.9 us
    pallas_call x1, Pallas kernels, on_device(): pl.pallas_call(functools.partial(up_kernel, n_head, n_expert, split, grou...  10.8 us
    ppermute x6, starting transfers between devices, shift(): lax.ppermute(value, 'expert', [(i, (i + k) % n_expert) for i in range(n_e...  6.77 us
  transfers between devices with their start and end apart: 24, of which 10 were waited for; matrix products, arithmetic and copies ran while one was open for 0% of the time, Pallas kernels for 11%

profile of v2, /device:TPU:0, one launch (start us, length us, event | category | flops | bytes accessed | tf_op | source)
XLA Modules:
  0.0 75.6 jit_solution(10626396439680359590)
XLA Ops:
  0.0 0.0 slice-start.1
  0.0 0.0 slice-start.2
  0.0 1.1 %pack.1.refs_0_ = bf16[144,512]{1,0:T(8,128)(2,1)S(1)} custom-call(bf16[128,512]{1,0:T(8,128)(2,1)} %rows_hbm.1, bf16[512]{0:T(512)(128)(2,1)} %gain_hbm.1, s32[8,128]{1,0:T(8,128)} %bitcast.8, f32[8,128]{1,0:T(8,128)} %bitcast.9, bf16[16,2048,256]{2,1,0:T(8,128)(2,1)} %refs_16_.1, bf16[16,2048,256]{2,1,0:T(8,128)(2,1)} %refs_17_.1, ...), custom_call_target="tpu_custom_call" | custom-call | tf_op jit(solution)/shard_map/pack/pallas_call | solution.py:206
  1.2 3.0 %collective-permute-start.7 = (bf16[144,512]{1,0:T(8,128)(2,1)S(1)}, bf16[144,512]{1,0:T(8,128)(2,1)S(1)}, u32[]{:S(2)}, u32[]{:S(2)}) collective-permute-start(bf16[144,512]{1,0:T(8,128)(2,1)S(1)} %pack.1.refs_0_), channel_id=1, source_target_pairs={{0,2},{1,3},{2,0},{3,1},{4,6},{5,7},{6,4},{7,5},{8,10},{9,11},{10,... | collective-permute-start | bytes 442376 | tf_op jit(solution)/shard_map/ppermute | solution.py:222
  4.2 3.6 %collective-permute-start.2 = (bf16[144,512]{1,0:T(8,128)(2,1)S(1)}, bf16[144,512]{1,0:T(8,128)(2,1)S(1)}, u32[]{:S(2)}, u32[]{:S(2)}) collective-permute-start(bf16[144,512]{1,0:T(8,128)(2,1)S(1)} %pack.1.refs_0_), channel_id=1, source_target_pairs={{0,12},{4,0},{8,4},{12,8},{1,13},{5,1},{9,5},{13,9},{2,14},{6,2},{... | collective-permute-start | bytes 442376 | tf_op jit(solution)/shard_map/ppermute | solution.py:225
  7.8 0.0 collective-permute-start.3
  7.8 0.0 collective-permute-start.1
  7.8 1.0 %collective-permute-start = (bf16[144,512]{1,0:T(8,128)(2,1)S(1)}, bf16[144,512]{1,0:T(8,128)(2,1)S(1)}, u32[]{:S(2)}, u32[]{:S(2)}) collective-permute-start(bf16[144,512]{1,0:T(8,128)(2,1)S(1)} %pack.1.refs_0_), channel_id=1, source_target_pairs={{0,4},{4,8},{8,12},{12,0},{1,5},{5,9},{9,13},{13,1},{2,6},{6,10},{... | collective-permute-start | bytes 442376 | tf_op jit(solution)/shard_map/ppermute | solution.py:225
  8.8 0.0 collective-permute-done.7.refs_8_
  8.8 0.0 collective-permute-start.11
  8.8 3.3 %collective-permute-done.2.refs_3_ = bf16[144,512]{1,0:T(8,128)(2,1)S(1)} collective-permute-done((bf16[144,512]{1,0:T(8,128)(2,1)S(1)}, bf16[144,512]{1,0:T(8,128)(2,1)S(1)}, u32[]{:S(2)}, u32[]{:S(2)}) %collective-permute-start.2) | collective-permute-done | bytes 147488 | tf_op jit(solution)/shard_map/ppermute | solution.py:225
  12.1 0.5 collective-permute-start.10
  12.6 0.0 collective-permute-done.3.refs_4_
  12.6 0.0 collective-permute-start.6
  12.6 7.8 %collective-permute-done.1.refs_2_ = bf16[144,512]{1,0:T(8,128)(2,1)S(1)} collective-permute-done((bf16[144,512]{1,0:T(8,128)(2,1)S(1)}, bf16[144,512]{1,0:T(8,128)(2,1)S(1)}, u32[]{:S(2)}, u32[]{:S(2)}) %collective-permute-start.1) | collective-permute-done | bytes 147488 | tf_op jit(solution)/shard_map/ppermute | solution.py:225
  20.4 0.5 collective-permute-start.9
  21.0 0.0 collective-permute-done.refs_1_
  21.0 1.5 %collective-permute-start.8 = (bf16[144,512]{1,0:T(8,128)(2,1)S(1)}, bf16[144,512]{1,0:T(8,128)(2,1)S(1)}, u32[]{:S(2)}, u32[]{:S(2)}) collective-permute-start(bf16[144,512]{1,0:T(8,128)(2,1)S(1)} %collective-permute-done.refs_1_), channel_id=1, source_target_pairs={{0,2},{1,3},{2,0},{3,1},{4,6},{5,7},{6,4},{7,5},{8,10},{9,11},{10,... | collective-permute-start | bytes 442376 | tf_op jit(solution)/shard_map/ppermute | solution.py:222
  22.5 0.0 collective-permute-done.11.refs_12_
  22.5 0.0 collective-permute-start.5
  22.5 0.0 collective-permute-done.10.refs_11_
  22.5 0.5 collective-permute-start.4
  23.0 0.0 collective-permute-done.6.refs_7_
  23.0 0.1 collective-permute-start.14
  23.1 4.1 %collective-permute-done.9.refs_10_ = bf16[144,512]{1,0:T(8,128)(2,1)S(1)} collective-permute-done((bf16[144,512]{1,0:T(8,128)(2,1)S(1)}, bf16[144,512]{1,0:T(8,128)(2,1)S(1)}, u32[]{:S(2)}, u32[]{:S(2)}) %collective-permute-start.9) | collective-permute-done | bytes 147488 | tf_op jit(solution)/shard_map/ppermute | solution.py:222
  27.2 0.0 collective-permute-start.13
  27.2 2.1 %collective-permute-done.8.refs_9_ = bf16[144,512]{1,0:T(8,128)(2,1)S(1)} collective-permute-done((bf16[144,512]{1,0:T(8,128)(2,1)S(1)}, bf16[144,512]{1,0:T(8,128)(2,1)S(1)}, u32[]{:S(2)}, u32[]{:S(2)}) %collective-permute-start.8) | collective-permute-done | bytes 147488 | tf_op jit(solution)/shard_map/ppermute | solution.py:222
  29.2 0.0 collective-permute-start.12
  29.2 0.0 collective-permute-done.5.refs_6_
  29.3 0.0 collective-permute-done.4.refs_5_
  29.3 0.0 collective-permute-done.14.refs_15_
  29.3 0.0 collective-permute-done.13.refs_14_
  29.3 1.3 %collective-permute-done.12.refs_13_ = bf16[144,512]{1,0:T(8,128)(2,1)S(1)} collective-permute-done((bf16[144,512]{1,0:T(8,128)(2,1)S(1)}, bf16[144,512]{1,0:T(8,128)(2,1)S(1)}, u32[]{:S(2)}, u32[]{:S(2)}) %collective-permute-start.12) | collective-permute-done | bytes 147488 | tf_op jit(solution)/shard_map/ppermute | solution.py:222
  30.6 0.0 copy-done.1
  30.6 0.0 slice-start.3
  30.7 0.0 copy-start.2
  30.7 10.8 %up.1 = (bf16[16,96,256]{2,1,0:T(8,128)(2,1)S(1)}, bf16[2,256,768]{2,1,0:T(8,128)(2,1)S(1)}) custom-call(s32[16,2,16]{2,1,0:T(2,128)S(1)} %bitcast.6, s32[16,2,16]{2,1,0:T(2,128)S(1)} %bitcast.7, bf16[144,512]{1,0:T(8,128)(2,1)S(1)} %pack.1.refs_0_, bf16[144,512]{1,0:T(8,128)(2,1)S(1)} %collective-permute-done.refs_1_, ...), custom_call_target="tpu_custom_call" | custom-call | tf_op jit(solution)/shard_map/up/pallas_call | solution.py:239
  41.5 0.0 slice-done
  41.6 2.8 %down3.1 = bf16[512,512]{1,0:T(8,128)(2,1)S(1)} custom-call(s32[16,2,16]{2,1,0:T(2,128)S(1)} %copy-done.2, bf16[16,96,256]{2,1,0:T(8,128)(2,1)S(1)} %get-tuple-element.15.act_ref, bf16[2,256,768]{2,1,0:T(8,128)(2,1)S(1)} %get-tuple-element.16.comb_ref, bf16[16,256,2048]{2,1,0:T(8,128)(2,1)S(1)} %bitcast.5), custom_call_target="tpu_custom_call" | custom-call | tf_op jit(solution)/shard_map/down3/pallas_call | solution.py:258
  44.3 0.2 collective-permute-start.16
  44.5 2.7 %down1.1 = bf16[512,512]{1,0:T(8,128)(2,1)S(1)} custom-call(s32[16,2,16]{2,1,0:T(2,128)S(1)} %copy-done.2, bf16[16,96,256]{2,1,0:T(8,128)(2,1)S(1)} %get-tuple-element.15.act_ref, bf16[2,256,768]{2,1,0:T(8,128)(2,1)S(1)} %get-tuple-element.16.comb_ref, bf16[16,256,2048]{2,1,0:T(8,128)(2,1)S(1)} %bitcast.5), custom_call_target="tpu_custom_call" | custom-call | tf_op jit(solution)/shard_map/down1/pallas_call | solution.py:258
  47.3 0.0 copy-start.5
  47.3 0.4 collective-permute-start.15
  47.7 2.7 %down2.1 = (bf16[128,512]{1,0:T(8,128)(2,1)S(1)}, bf16[128,512]{1,0:T(8,128)(2,1)S(1)}, bf16[128,512]{1,0:T(8,128)(2,1)S(1)}, bf16[128,512]{1,0:T(8,128)(2,1)S(1)}) custom-call(s32[16,2,16]{2,1,0:T(2,128)S(1)} %copy-done.2, bf16[16,96,256]{2,1,0:T(8,128)(2,1)S(1)} %get-tuple-element.15.act_ref, bf16[2,256,768]{2,1,0:T(8,128)(2,1)S(1)} %get-tuple-element.16.comb_ref, ...), custom_call_target="tpu_custom_call" | custom-call | tf_op jit(solution)/shard_map/down2/pallas_call | solution.py:258
  50.4 0.0 collective-permute-done.16
  50.5 0.1 add_convert_fusion.2
  50.6 0.6 collective-permute-start.21
  51.2 1.5 %collective-permute-start.19 = (bf16[128,512]{1,0:T(8,128)(2,1)S(1)}, bf16[128,512]{1,0:T(8,128)(2,1)S(1)}, u32[]{:S(2)}, u32[]{:S(2)}) collective-permute-start(bf16[128,512]{1,0:T(8,128)(2,1)S(1)} %get-tuple-element.27), channel_id=1, source_target_pairs={{0,2},{1,3},{2,0},{3,1},{4,6},{5,7},{6,4},{7,5},{8,10},{9,11},{10,... | collective-permute-start | bytes 393224 | tf_op jit(solution)/shard_map/ppermute | solution.py:222
  52.7 0.5 collective-permute-start.17
  53.2 2.7 %down0.1 = (bf16[128,512]{1,0:T(8,128)(2,1)S(1)}, bf16[128,512]{1,0:T(8,128)(2,1)S(1)}, bf16[128,512]{1,0:T(8,128)(2,1)S(1)}, bf16[128,512]{1,0:T(8,128)(2,1)S(1)}) custom-call(s32[16,2,16]{2,1,0:T(2,128)S(1)} %copy-done.2, bf16[16,96,256]{2,1,0:T(8,128)(2,1)S(1)} %get-tuple-element.15.act_ref, bf16[2,256,768]{2,1,0:T(8,128)(2,1)S(1)} %get-tuple-element.16.comb_ref, ...), custom_call_target="tpu_custom_call" | custom-call | tf_op jit(solution)/shard_map/down0/pallas_call | solution.py:258
  55.9 1.6 %collective-permute-start.23 = (bf16[128,512]{1,0:T(8,128)(2,1)S(1)}, bf16[128,512]{1,0:T(8,128)(2,1)S(1)}, u32[]{:S(2)}, u32[]{:S(2)}) collective-permute-start(bf16[128,512]{1,0:T(8,128)(2,1)S(1)} %get-tuple-element.25), channel_id=1, source_target_pairs={{0,2},{1,3},{2,0},{3,1},{4,6},{5,7},{6,4},{7,5},{8,10},{9,11},{10,... | collective-permute-start | bytes 393224 | tf_op jit(solution)/shard_map/ppermute | solution.py:222
  57.5 0.0 collective-permute-done.15
  57.5 0.0 collective-permute-done.21
  57.5 2.3 %collective-permute-done.19 = bf16[128,512]{1,0:T(8,128)(2,1)S(1)} collective-permute-done((bf16[128,512]{1,0:T(8,128)(2,1)S(1)}, bf16[128,512]{1,0:T(8,128)(2,1)S(1)}, u32[]{:S(2)}, u32[]{:S(2)}) %collective-permute-start.19) | collective-permute-done | bytes 131104 | tf_op jit(solution)/shard_map/ppermute | solution.py:222
  59.8 2.8 %collective-permute-done.17 = bf16[128,512]{1,0:T(8,128)(2,1)S(1)} collective-permute-done((bf16[128,512]{1,0:T(8,128)(2,1)S(1)}, bf16[128,512]{1,0:T(8,128)(2,1)S(1)}, u32[]{:S(2)}, u32[]{:S(2)}) %collective-permute-start.17) | collective-permute-done | bytes 131104 | tf_op jit(solution)/shard_map/ppermute | solution.py:222
  62.6 0.2 add_convert_fusion.7
  62.8 1.0 %collective-permute-start.18 = (bf16[128,512]{1,0:T(8,128)(2,1)S(1)}, bf16[128,512]{1,0:T(8,128)(2,1)S(1)}, u32[]{:S(2)}, u32[]{:S(2)}) collective-permute-start(bf16[128,512]{1,0:T(8,128)(2,1)S(1)} %get-tuple-element.29), channel_id=1, source_target_pairs={{0,12},{4,0},{8,4},{12,8},{1,13},{5,1},{9,5},{13,9},{2,14},{6,2},{... | collective-permute-start | bytes 393224 | tf_op jit(solution)/shard_map/ppermute | solution.py:225
  63.8 1.1 %collective-permute-start.22 = (bf16[128,512]{1,0:T(8,128)(2,1)S(1)}, bf16[128,512]{1,0:T(8,128)(2,1)S(1)}, u32[]{:S(2)}, u32[]{:S(2)}) collective-permute-start(bf16[128,512]{1,0:T(8,128)(2,1)S(1)} %get-tuple-element.30), channel_id=1, source_target_pairs={{0,4},{4,8},{8,12},{12,0},{1,5},{5,9},{9,13},{13,1},{2,6},{6,10},{... | collective-permute-start | bytes 393224 | tf_op jit(solution)/shard_map/ppermute | solution.py:225
  64.9 0.1 collective-permute-start.20
  65.0 0.0 collective-permute-done.23
  65.0 6.1 %collective-permute-done.18 = bf16[128,512]{1,0:T(8,128)(2,1)S(1)} collective-permute-done((bf16[128,512]{1,0:T(8,128)(2,1)S(1)}, bf16[128,512]{1,0:T(8,128)(2,1)S(1)}, u32[]{:S(2)}, u32[]{:S(2)}) %collective-permute-start.18) | collective-permute-done | bytes 131104 | tf_op jit(solution)/shard_map/ppermute | solution.py:225
  71.0 0.5 collective-permute-done.22
  71.6 3.2 %collective-permute-done.20 = bf16[128,512]{1,0:T(8,128)(2,1)S(1)} collective-permute-done((bf16[128,512]{1,0:T(8,128)(2,1)S(1)}, bf16[128,512]{1,0:T(8,128)(2,1)S(1)}, u32[]{:S(2)}, u32[]{:S(2)}) %collective-permute-start.20) | collective-permute-done | bytes 131104 | tf_op jit(solution)/shard_map/ppermute | solution.py:225
  74.8 0.8 %add_convert_fusion = bf16[128,512]{1,0:T(8,128)(2,1)} fusion(bf16[128,512]{1,0:T(8,128)(2,1)S(1)} %collective-permute-done.22, bf16[128,512]{1,0:T(8,128)(2,1)S(1)} %collective-permute-done.20, bf16[128,512]{1,0:T(8,128)(2,1)S(1)} %collective-permute-done.18, bf16[128,512]{1,0:T(8,128)(2,1)S(1)} %copy-done.5, bf16[128,512]{1,0:T(8,128)(2,1)S(1)} %collective-permute-done.23, ...), kind=kLoop, calls=%fused_computation | loop fusion | flops 1048576 | bytes 1048576 | tf_op jit(solution)/shard_map/convert_element_type | solution.py:293
  (14 shorter events, 0.0 us)
Async XLA Ops:
  0.0 30.6 %copy-start = (bf16[16,2048,256]{2,1,0:T(8,128)(2,1)S(1)}, bf16[16,2048,256]{2,1,0:T(8,128)(2,1)}, u32[]{:S(2)}) copy-start(bf16[16,2048,256]{2,1,0:T(8,128)(2,1)} %refs_16_.1) | copy-start | bytes 50331652
  0.0 30.6 %copy-start.1 = (bf16[16,2048,256]{2,1,0:T(8,128)(2,1)S(1)}, bf16[16,2048,256]{2,1,0:T(8,128)(2,1)}, u32[]{:S(2)}) copy-start(bf16[16,2048,256]{2,1,0:T(8,128)(2,1)} %refs_17_.1) | copy-start | bytes 50331652
  0.0 30.6 %copy-start.3 = (s32[16,16,2]{1,2,0:T(2,128)S(1)}, s32[16,16,2]{1,2,0:T(2,128)}, u32[]{:S(2)}) copy-start(s32[16,16,2]{1,2,0:T(2,128)} %param.17) | copy-start | bytes 6148
  0.0 30.6 %copy-start.4 = (s32[16,16,2]{1,2,0:T(2,128)S(1)}, s32[16,16,2]{1,2,0:T(2,128)}, u32[]{:S(2)}) copy-start(s32[16,16,2]{1,2,0:T(2,128)} %param.18) | copy-start | bytes 6148
  0.0 41.5 %slice-start = ((s8[16777216]{0:T(1024)(128)(4,1)}), s8[4194304]{0:T(1024)(128)(4,1)S(1)}, s32[]{:S(2)}) async-start(s8[16777216]{0:T(1024)(128)(4,1)} %bitcast.4), calls=%async_computation | async-start | bytes 8388608
  0.0 41.5 %slice-start.1 = ((s8[16777216]{0:T(1024)(128)(4,1)}), s8[4194304]{0:T(1024)(128)(4,1)S(1)}, s32[]{:S(2)}) async-start(s8[16777216]{0:T(1024)(128)(4,1)} %bitcast.4), calls=%async_computation.1 | async-start | bytes 8388608
  0.0 41.5 %slice-start.2 = ((s8[16777216]{0:T(1024)(128)(4,1)}), s8[4194304]{0:T(1024)(128)(4,1)S(1)}, s32[]{:S(2)}) async-start(s8[16777216]{0:T(1024)(128)(4,1)} %bitcast.4), calls=%async_computation.2 | async-start | bytes 8388608
  1.2 7.7 %collective-permute-start.7 = (bf16[144,512]{1,0:T(8,128)(2,1)S(1)}, bf16[144,512]{1,0:T(8,128)(2,1)S(1)}, u32[]{:S(2)}, u32[]{:S(2)}) collective-permute-start(bf16[144,512]{1,0:T(8,128)(2,1)S(1)} %pack.1.refs_0_), channel_id=1, source_target_pairs={{0,2},{1,3},{2,0},{3,1},{4,6},{5,7},{6,4},{7,5},{8,10},{9,11},{10,... | collective-permute-start | bytes 442376 | tf_op jit(solution)/shard_map/ppermute | solution.py:222
  4.2 7.9 %collective-permute-start.2 = (bf16[144,512]{1,0:T(8,128)(2,1)S(1)}, bf16[144,512]{1,0:T(8,128)(2,1)S(1)}, u32[]{:S(2)}, u32[]{:S(2)}) collective-permute-start(bf16[144,512]{1,0:T(8,128)(2,1)S(1)} %pack.1.refs_0_), channel_id=1, source_target_pairs={{0,12},{4,0},{8,4},{12,8},{1,13},{5,1},{9,5},{13,9},{2,14},{6,2},{... | collective-permute-start | bytes 442376 | tf_op jit(solution)/shard_map/ppermute | solution.py:225
  7.8 4.8 %collective-permute-start.3 = (bf16[144,512]{1,0:T(8,128)(2,1)S(1)}, bf16[144,512]{1,0:T(8,128)(2,1)S(1)}, u32[]{:S(2)}, u32[]{:S(2)}) collective-permute-start(bf16[144,512]{1,0:T(8,128)(2,1)S(1)} %pack.1.refs_0_), channel_id=1, source_target_pairs={{0,1},{1,0},{2,3},{3,2},{4,5},{5,4},{6,7},{7,6},{8,9},{9,8},{10,11... | collective-permute-start | bytes 442376 | tf_op jit(solution)/shard_map/ppermute | solution.py:222
  7.8 12.6 %collective-permute-start.1 = (bf16[144,512]{1,0:T(8,128)(2,1)S(1)}, bf16[144,512]{1,0:T(8,128)(2,1)S(1)}, u32[]{:S(2)}, u32[]{:S(2)}) collective-permute-start(bf16[144,512]{1,0:T(8,128)(2,1)S(1)} %pack.1.refs_0_), channel_id=1, source_target_pairs={{0,8},{4,12},{8,0},{12,4},{1,9},{5,13},{9,1},{13,5},{2,10},{6,14},... | collective-permute-start | bytes 442376 | tf_op jit(solution)/shard_map/ppermute | solution.py:225
  7.8 13.2 %collective-permute-start = (bf16[144,512]{1,0:T(8,128)(2,1)S(1)}, bf16[144,512]{1,0:T(8,128)(2,1)S(1)}, u32[]{:S(2)}, u32[]{:S(2)}) collective-permute-start(bf16[144,512]{1,0:T(8,128)(2,1)S(1)} %pack.1.refs_0_), channel_id=1, source_target_pairs={{0,4},{4,8},{8,12},{12,0},{1,5},{5,9},{9,13},{13,1},{2,6},{6,10},{... | collective-permute-start | bytes 442376 | tf_op jit(solution)/shard_map/ppermute | solution.py:225
  8.8 13.7 %collective-permute-start.11 = (bf16[144,512]{1,0:T(8,128)(2,1)S(1)}, bf16[144,512]{1,0:T(8,128)(2,1)S(1)}, u32[]{:S(2)}, u32[]{:S(2)}) collective-permute-start(bf16[144,512]{1,0:T(8,128)(2,1)S(1)} %collective-permute-done.7.refs_8_), channel_id=1, source_target_pairs={{0,1},{1,0},{2,3},{3,2},{4,5},{5,4},{6,7},{7,6},{8,9},{9,8},{10,11... | collective-permute-start | bytes 442376 | tf_op jit(solution)/shard_map/ppermute | solution.py:222
  12.1 10.4 %collective-permute-start.10 = (bf16[144,512]{1,0:T(8,128)(2,1)S(1)}, bf16[144,512]{1,0:T(8,128)(2,1)S(1)}, u32[]{:S(2)}, u32[]{:S(2)}) collective-permute-start(bf16[144,512]{1,0:T(8,128)(2,1)S(1)} %collective-permute-done.2.refs_3_), channel_id=1, source_target_pairs={{0,2},{1,3},{2,0},{3,1},{4,6},{5,7},{6,4},{7,5},{8,10},{9,11},{10,... | collective-permute-start | bytes 442376 | tf_op jit(solution)/shard_map/ppermute | solution.py:222
  12.6 10.4 %collective-permute-start.6 = (bf16[144,512]{1,0:T(8,128)(2,1)S(1)}, bf16[144,512]{1,0:T(8,128)(2,1)S(1)}, u32[]{:S(2)}, u32[]{:S(2)}) collective-permute-start(bf16[144,512]{1,0:T(8,128)(2,1)S(1)} %collective-permute-done.2.refs_3_), channel_id=1, source_target_pairs={{0,1},{1,0},{2,3},{3,2},{4,5},{5,4},{6,7},{7,6},{8,9},{9,8},{10,11... | collective-permute-start | bytes 442376 | tf_op jit(solution)/shard_map/ppermute | solution.py:222
  20.4 6.7 %collective-permute-start.9 = (bf16[144,512]{1,0:T(8,128)(2,1)S(1)}, bf16[144,512]{1,0:T(8,128)(2,1)S(1)}, u32[]{:S(2)}, u32[]{:S(2)}) collective-permute-start(bf16[144,512]{1,0:T(8,128)(2,1)S(1)} %collective-permute-done.1.refs_2_), channel_id=1, source_target_pairs={{0,2},{1,3},{2,0},{3,1},{4,6},{5,7},{6,4},{7,5},{8,10},{9,11},{10,... | collective-permute-start | bytes 442376 | tf_op jit(solution)/shard_map/ppermute | solution.py:222
  21.0 8.3 %collective-permute-start.8 = (bf16[144,512]{1,0:T(8,128)(2,1)S(1)}, bf16[144,512]{1,0:T(8,128)(2,1)S(1)}, u32[]{:S(2)}, u32[]{:S(2)}) collective-permute-start(bf16[144,512]{1,0:T(8,128)(2,1)S(1)} %collective-permute-done.refs_1_), channel_id=1, source_target_pairs={{0,2},{1,3},{2,0},{3,1},{4,6},{5,7},{6,4},{7,5},{8,10},{9,11},{10,... | collective-permute-start | bytes 442376 | tf_op jit(solution)/shard_map/ppermute | solution.py:222
  22.5 6.8 %collective-permute-start.5 = (bf16[144,512]{1,0:T(8,128)(2,1)S(1)}, bf16[144,512]{1,0:T(8,128)(2,1)S(1)}, u32[]{:S(2)}, u32[]{:S(2)}) collective-permute-start(bf16[144,512]{1,0:T(8,128)(2,1)S(1)} %collective-permute-done.1.refs_2_), channel_id=1, source_target_pairs={{0,1},{1,0},{2,3},{3,2},{4,5},{5,4},{6,7},{7,6},{8,9},{9,8},{10,11... | collective-permute-start | bytes 442376 | tf_op jit(solution)/shard_map/ppermute | solution.py:222
  22.5 6.8 %collective-permute-start.4 = (bf16[144,512]{1,0:T(8,128)(2,1)S(1)}, bf16[144,512]{1,0:T(8,128)(2,1)S(1)}, u32[]{:S(2)}, u32[]{:S(2)}) collective-permute-start(bf16[144,512]{1,0:T(8,128)(2,1)S(1)} %collective-permute-done.refs_1_), channel_id=1, source_target_pairs={{0,1},{1,0},{2,3},{3,2},{4,5},{5,4},{6,7},{7,6},{8,9},{9,8},{10,11... | collective-permute-start | bytes 442376 | tf_op jit(solution)/shard_map/ppermute | solution.py:222
  23.0 6.3 %collective-permute-start.14 = (bf16[144,512]{1,0:T(8,128)(2,1)S(1)}, bf16[144,512]{1,0:T(8,128)(2,1)S(1)}, u32[]{:S(2)}, u32[]{:S(2)}) collective-permute-start(bf16[144,512]{1,0:T(8,128)(2,1)S(1)} %collective-permute-done.10.refs_11_), channel_id=1, source_target_pairs={{0,1},{1,0},{2,3},{3,2},{4,5},{5,4},{6,7},{7,6},{8,9},{9,8},{10,11... | collective-permute-start | bytes 442376 | tf_op jit(solution)/shard_map/ppermute | solution.py:222
  27.2 2.1 %collective-permute-start.13 = (bf16[144,512]{1,0:T(8,128)(2,1)S(1)}, bf16[144,512]{1,0:T(8,128)(2,1)S(1)}, u32[]{:S(2)}, u32[]{:S(2)}) collective-permute-start(bf16[144,512]{1,0:T(8,128)(2,1)S(1)} %collective-permute-done.9.refs_10_), channel_id=1, source_target_pairs={{0,1},{1,0},{2,3},{3,2},{4,5},{5,4},{6,7},{7,6},{8,9},{9,8},{10,11... | collective-permute-start | bytes 442376 | tf_op jit(solution)/shard_map/ppermute | solution.py:222
  29.2 1.4 %collective-permute-start.12 = (bf16[144,512]{1,0:T(8,128)(2,1)S(1)}, bf16[144,512]{1,0:T(8,128)(2,1)S(1)}, u32[]{:S(2)}, u32[]{:S(2)}) collective-permute-start(bf16[144,512]{1,0:T(8,128)(2,1)S(1)} %collective-permute-done.8.refs_9_), channel_id=1, source_target_pairs={{0,1},{1,0},{2,3},{3,2},{4,5},{5,4},{6,7},{7,6},{8,9},{9,8},{10,11... | collective-permute-start | bytes 442376 | tf_op jit(solution)/shard_map/ppermute | solution.py:222
  30.6 10.9 %slice-start.3 = ((s8[16777216]{0:T(1024)(128)(4,1)}), s8[4194304]{0:T(1024)(128)(4,1)S(1)}, s32[]{:S(2)}) async-start(s8[16777216]{0:T(1024)(128)(4,1)} %bitcast.4), calls=%async_computation.3 | async-start | bytes 8388608
  30.7 10.9 %copy-start.2 = (s32[16,2,16]{2,1,0:T(2,128)S(1)}, s32[16,2,16]{2,1,0:T(2,128)}, u32[]{:S(2)}) copy-start(s32[16,2,16]{2,1,0:T(2,128)} %down_exp.7) | copy-start | bytes 6148
  44.3 6.1 %collective-permute-start.16 = (bf16[512,512]{1,0:T(8,128)(2,1)S(1)}, bf16[512,512]{1,0:T(8,128)(2,1)S(1)}, u32[]{:S(2)}, u32[]{:S(2)}) collective-permute-start(bf16[512,512]{1,0:T(8,128)(2,1)S(1)} %down3.1), channel_id=1, source_target_pairs={{0,1},{1,0},{2,3},{3,2},{4,5},{5,4},{6,7},{7,6},{8,9},{9,8},{10,11... | collective-permute-start | bytes 1572872 | tf_op jit(solution)/shard_map/ppermute | solution.py:222
  47.3 27.5 %copy-start.5 = (bf16[128,512]{1,0:T(8,128)(2,1)S(1)}, bf16[128,512]{1,0:T(8,128)(2,1)}, u32[]{:S(2)}) copy-start(bf16[128,512]{1,0:T(8,128)(2,1)} %rows_hbm.1) | copy-start | bytes 393220
  47.3 10.2 %collective-permute-start.15 = (bf16[512,512]{1,0:T(8,128)(2,1)S(1)}, bf16[512,512]{1,0:T(8,128)(2,1)S(1)}, u32[]{:S(2)}, u32[]{:S(2)}) collective-permute-start(bf16[512,512]{1,0:T(8,128)(2,1)S(1)} %down1.1), channel_id=1, source_target_pairs={{0,1},{1,0},{2,3},{3,2},{4,5},{5,4},{6,7},{7,6},{8,9},{9,8},{10,11... | collective-permute-start | bytes 1572872 | tf_op jit(solution)/shard_map/ppermute | solution.py:222
  50.6 6.9 %collective-permute-start.21 = (bf16[128,512]{1,0:T(8,128)(2,1)S(1)}, bf16[128,512]{1,0:T(8,128)(2,1)S(1)}, u32[]{:S(2)}, u32[]{:S(2)}) collective-permute-start(bf16[128,512]{1,0:T(8,128)(2,1)S(1)} %get-tuple-element.26), channel_id=1, source_target_pairs={{0,2},{1,3},{2,0},{3,1},{4,6},{5,7},{6,4},{7,5},{8,10},{9,11},{10,... | collective-permute-start | bytes 393224 | tf_op jit(solution)/shard_map/ppermute | solution.py:222
  51.2 8.6 %collective-permute-start.19 = (bf16[128,512]{1,0:T(8,128)(2,1)S(1)}, bf16[128,512]{1,0:T(8,128)(2,1)S(1)}, u32[]{:S(2)}, u32[]{:S(2)}) collective-permute-start(bf16[128,512]{1,0:T(8,128)(2,1)S(1)} %get-tuple-element.27), channel_id=1, source_target_pairs={{0,2},{1,3},{2,0},{3,1},{4,6},{5,7},{6,4},{7,5},{8,10},{9,11},{10,... | collective-permute-start | bytes 393224 | tf_op jit(solution)/shard_map/ppermute | solution.py:222
  52.7 10.0 %collective-permute-start.17 = (bf16[128,512]{1,0:T(8,128)(2,1)S(1)}, bf16[128,512]{1,0:T(8,128)(2,1)S(1)}, u32[]{:S(2)}, u32[]{:S(2)}) collective-permute-start(bf16[128,512]{1,0:T(8,128)(2,1)S(1)} %get-tuple-element.28), channel_id=1, source_target_pairs={{0,2},{1,3},{2,0},{3,1},{4,6},{5,7},{6,4},{7,5},{8,10},{9,11},{10,... | collective-permute-start | bytes 393224 | tf_op jit(solution)/shard_map/ppermute | solution.py:222
  55.9 9.0 %collective-permute-start.23 = (bf16[128,512]{1,0:T(8,128)(2,1)S(1)}, bf16[128,512]{1,0:T(8,128)(2,1)S(1)}, u32[]{:S(2)}, u32[]{:S(2)}) collective-permute-start(bf16[128,512]{1,0:T(8,128)(2,1)S(1)} %get-tuple-element.25), channel_id=1, source_target_pairs={{0,2},{1,3},{2,0},{3,1},{4,6},{5,7},{6,4},{7,5},{8,10},{9,11},{10,... | collective-permute-start | bytes 393224 | tf_op jit(solution)/shard_map/ppermute | solution.py:222
  62.8 8.2 %collective-permute-start.18 = (bf16[128,512]{1,0:T(8,128)(2,1)S(1)}, bf16[128,512]{1,0:T(8,128)(2,1)S(1)}, u32[]{:S(2)}, u32[]{:S(2)}) collective-permute-start(bf16[128,512]{1,0:T(8,128)(2,1)S(1)} %get-tuple-element.29), channel_id=1, source_target_pairs={{0,12},{4,0},{8,4},{12,8},{1,13},{5,1},{9,5},{13,9},{2,14},{6,2},{... | collective-permute-start | bytes 393224 | tf_op jit(solution)/shard_map/ppermute | solution.py:225
  63.8 7.7 %collective-permute-start.22 = (bf16[128,512]{1,0:T(8,128)(2,1)S(1)}, bf16[128,512]{1,0:T(8,128)(2,1)S(1)}, u32[]{:S(2)}, u32[]{:S(2)}) collective-permute-start(bf16[128,512]{1,0:T(8,128)(2,1)S(1)} %get-tuple-element.30), channel_id=1, source_target_pairs={{0,4},{4,8},{8,12},{12,0},{1,5},{5,9},{9,13},{13,1},{2,6},{6,10},{... | collective-permute-start | bytes 393224 | tf_op jit(solution)/shard_map/ppermute | solution.py:225
  64.9 9.9 %collective-permute-start.20 = (bf16[128,512]{1,0:T(8,128)(2,1)S(1)}, bf16[128,512]{1,0:T(8,128)(2,1)S(1)}, u32[]{:S(2)}, u32[]{:S(2)}) collective-permute-start(bf16[128,512]{1,0:T(8,128)(2,1)S(1)} %get-tuple-element.31), channel_id=1, source_target_pairs={{0,8},{4,12},{8,0},{12,4},{1,9},{5,13},{9,1},{13,5},{2,10},{6,14},... | collective-permute-start | bytes 393224 | tf_op jit(solution)/shard_map/ppermute | solution.py:225
